TPU v7x, 32 devices: a whole 2x2x4 slice. The times are simulated.
32 devices in a mesh: ctx: 8 (over y, x, core), fsdp: 4 (over z).
Axes of the slice: x: 2, y: 2, z: 4, core: 2. Of those that a mesh axis runs over, the one named last changes fastest.
Arguments:
- xbc: bfloat16 [4, 1024, 9216], P('fsdp', 'ctx'), may hold values from -6 to 6
- dt_raw: bfloat16 [4, 128, 1024], P('fsdp', None, 'ctx'), may hold values from -4 to 15
- dy: bfloat16 [4, 1024, 8192], P('fsdp', 'ctx'), may hold values from -6 to 6
- conv_params: float32 [5, 9216], replicated, may hold values from -3 to 3
- head_params: float32 [3, 128], replicated, may hold values from -13 to 1.5, as said below
Outputs:
- d_xbc: bfloat16 [4, 1024, 9216], P('fsdp', 'ctx')
- d_dt_raw: float32 [4, 128, 1024], P('fsdp', None, 'ctx')
- d_conv: float32 [5, 9216], replicated
- d_head: float32 [3, 128], replicated
Inputs may be any that keep to these rules, and one draw needn't show every extreme that they name: `head_params`: head parameters.
All inputs are finite; a program needn't handle non-finite values.
Results may differ from a plain program's by a relative error of at most 0.007.
Values may be sent and summed in bfloat16 or wider, within the bound.
A program may use at most 256 MiB of HBM per device.

v0:
```python
import jax
import jax.numpy as jnp
from jax import lax
from jax.sharding import PartitionSpec as P

HEADS = 128
HEAD_DIM = 64
STATE = 128
GROUPS = 4
CONV_W = 4
SPAN = 128


exact_prec = lax.Precision.HIGHEST


def shifted(block, axis, distance):
    devices = range(lax.axis_size(axis))
    route = [(i - distance, i) for i in devices if i - distance in devices]
    return lax.ppermute(block, axis, route)


def entering_2(value, axis, join, neutral, backward):
    count = lax.axis_size(axis)
    place = lax.axis_index(axis)
    ahead = count - 1 - place if backward else place
    gathered = jax.tree.map(
        lambda a, kind: lax.all_gather(a.astype(kind), axis), value, (jnp.bfloat16, jnp.bfloat16)
    )
    state = jax.tree.map(lambda a, e: jnp.zeros_like(a) + jnp.asarray(e, a.dtype), value, neutral)

    def one(hop, state):
        source = count - 1 - hop if backward else hop
        return join(
            state,
            jax.tree.map(
                lambda a, own: lax.dynamic_index_in_dim(a, source, 0, False).astype(own.dtype),
                gathered,
                value,
            ),
        )

    return lax.fori_loop(0, ahead, one, state)


def split_channels(activated):
    row_count = activated.shape[0]
    x_width = HEADS * HEAD_DIM
    bc_width = GROUPS * STATE
    x_heads = activated[:, :x_width].reshape(row_count, HEADS, HEAD_DIM)
    b_groups = activated[:, x_width : x_width + bc_width].reshape(row_count, GROUPS, STATE)
    c_groups = activated[:, x_width + bc_width :].reshape(row_count, GROUPS, STATE)
    return (x_heads, b_groups, c_groups)


def prepare(extended, dt_values, conv_params, head_params):
    row_count = extended.shape[0] - (CONV_W - 1)
    mixed_in = jnp.broadcast_to(conv_params[CONV_W][None, :], (row_count, extended.shape[1]))
    for offset in range(CONV_W):
        mixed_in = mixed_in + conv_params[offset][None, :] * extended[offset : offset + row_count]
    activated = jax.nn.silu(mixed_in)
    x_heads, b_groups, c_groups = split_channels(activated)
    step_size = jax.nn.softplus(dt_values + head_params[0][:, None])
    rates = step_size * jnp.exp(head_params[1])[:, None]
    return (x_heads, b_groups, c_groups, step_size, rates)


def span_outputs(x_heads, b_groups, c_groups, step_size, rates, head_params):
    row_count = x_heads.shape[0]
    block_count = row_count // SPAN
    per_group = HEADS // GROUPS
    x_blocks = x_heads.reshape(block_count, SPAN, HEADS, HEAD_DIM)
    b_blocks = b_groups.reshape(block_count, SPAN, GROUPS, STATE)
    c_blocks = c_groups.reshape(block_count, SPAN, GROUPS, STATE)
    d_blocks = step_size.reshape(HEADS, block_count, SPAN).transpose(1, 0, 2)
    l_blocks = rates.reshape(HEADS, block_count, SPAN).transpose(1, 0, 2)
    causal_mask = jnp.arange(SPAN)[:, None] >= jnp.arange(SPAN)[None, :]

    def advance(state_now, block):
        x_block, b_block, c_block, d_block, l_block = block
        running = jnp.cumsum(l_block, axis=1)
        spacing = jnp.where(causal_mask[None], running[:, :, None] - running[:, None, :], 0.0)
        fading = jnp.where(causal_mask[None], jnp.exp(-spacing), 0.0)
        scores = jnp.einsum("tgn,sgn->gts", c_block, b_block, precision=exact_prec)
        weights = (
            scores[:, None]
            * fading.reshape(GROUPS, per_group, SPAN, SPAN)
            * d_block.reshape(GROUPS, per_group, 1, SPAN)
        )
        x_grouped = x_block.reshape(SPAN, GROUPS, per_group, HEAD_DIM)
        outputs = jnp.einsum("gkts,sgkp->tgkp", weights, x_grouped, precision=exact_prec)
        carried = jnp.einsum(
            "tgn,gkpn->tgkp",
            c_block,
            state_now.reshape(GROUPS, per_group, HEAD_DIM, STATE),
            precision=exact_prec,
        )
        decay_rows = jnp.exp(-running).T.reshape(SPAN, GROUPS, per_group)[..., None]
        outputs = (outputs + carried * decay_rows).reshape(SPAN, HEADS, HEAD_DIM)
        tail_weight = (jnp.exp(running - running[:, -1:]) * d_block).T
        weighted = (tail_weight[:, :, None] * x_block).reshape(SPAN, GROUPS, per_group, HEAD_DIM)
        fresh_state = jnp.einsum("sgkp,sgn->gkpn", weighted, b_block, precision=exact_prec).reshape(
            HEADS, HEAD_DIM, STATE
        )
        state_next = jnp.exp(-running[:, -1])[:, None, None] * state_now + fresh_state
        return (state_next, outputs)

    initial = jnp.zeros((HEADS, HEAD_DIM, STATE), jnp.float32)
    _, outputs = lax.scan(advance, initial, (x_blocks, b_blocks, c_blocks, d_blocks, l_blocks))
    outputs = outputs.reshape(row_count, HEADS, HEAD_DIM) + head_params[2][None, :, None] * x_heads
    return outputs.reshape(row_count, HEADS * HEAD_DIM)


def end_state(x_heads, b_groups, step_size, rates):
    row_count = x_heads.shape[0]
    per_group = HEADS // GROUPS
    running = jnp.cumsum(rates, axis=1)
    tail_weight = (jnp.exp(running - running[:, -1:]) * step_size).T
    weighted = (tail_weight[:, :, None] * x_heads).reshape(row_count, GROUPS, per_group, HEAD_DIM)
    summed = jnp.einsum("sgkp,sgn->gkpn", weighted, b_groups, precision=exact_prec)
    return summed.reshape(HEADS, HEAD_DIM, STATE)


def entry_terms(c_groups, rates, entering):
    row_count = c_groups.shape[0]
    per_group = HEADS // GROUPS
    running = jnp.cumsum(rates, axis=1)
    carried = jnp.einsum(
        "tgn,gkpn->tgkp",
        c_groups,
        entering.reshape(GROUPS, per_group, HEAD_DIM, STATE),
        precision=exact_prec,
    )
    carried = carried * jnp.exp(-running).T.reshape(row_count, GROUPS, per_group)[..., None]
    passed = jnp.exp(-running[:, -1])[:, None, None] * entering
    return (carried.reshape(row_count, HEADS * HEAD_DIM), passed)


def state_pull(c_groups, rates, upstream_heads):
    row_count = c_groups.shape[0]
    per_group = HEADS // GROUPS
    running = jnp.cumsum(rates, axis=1)
    weighted = (jnp.exp(-running).T[:, :, None] * upstream_heads).reshape(
        row_count, GROUPS, per_group, HEAD_DIM
    )
    summed = jnp.einsum("tgkp,tgn->gkpn", weighted, c_groups, precision=exact_prec)
    return summed.reshape(HEADS, HEAD_DIM, STATE)


def combine_carry(earlier_pair, later_pair):
    return (
        earlier_pair[0] * later_pair[0],
        later_pair[0][:, None, None] * earlier_pair[1] + later_pair[1],
    )


def shards(xbc, dt_raw, dy, conv_params, head_params):
    rim_rows = CONV_W - 1
    row_count = xbc.shape[1]
    before = shifted(xbc[:, row_count - rim_rows :, :], "ctx", 1)
    extended = jnp.concatenate([before[0], xbc[0]], axis=0).astype(jnp.float32)
    pieces, prep_back = jax.vjp(
        prepare, extended, dt_raw[0].astype(jnp.float32), conv_params, head_params
    )
    x_heads, b_groups, c_groups, step_size, rates = pieces
    _, inner_back = jax.vjp(
        span_outputs, x_heads, b_groups, c_groups, step_size, rates, head_params
    )
    leaving_state, state_back = jax.vjp(end_state, x_heads, b_groups, step_size, rates)
    upstream = dy[0].astype(jnp.float32)
    pull_term = state_pull(c_groups, rates, upstream.reshape(row_count, HEADS, HEAD_DIM))
    fading = jnp.exp(-jnp.sum(rates, axis=1))
    identity_pair = (jnp.ones_like(fading), jnp.zeros_like(leaving_state))
    _, entering = entering_2((fading, leaving_state), "ctx", combine_carry, identity_pair, False)
    _, later_grad = entering_2((fading, pull_term), "ctx", combine_carry, identity_pair, True)
    _, entry_back = jax.vjp(entry_terms, c_groups, rates, entering)
    grad_x_inner, grad_b_inner, grad_c_inner, grad_step_inner, grad_rate_inner, grad_head_inner = (
        inner_back(upstream)
    )
    grad_x_state, grad_b_state, grad_step_state, grad_rate_state = state_back(later_grad)
    grad_c_entry, grad_rate_entry, _ = entry_back((upstream, later_grad))
    grad_ext, grad_dt, grad_conv, grad_head = prep_back(
        (
            grad_x_inner + grad_x_state,
            grad_b_inner + grad_b_state,
            grad_c_inner + grad_c_entry,
            grad_step_inner + grad_step_state,
            grad_rate_inner + grad_rate_state + grad_rate_entry,
        )
    )
    grad_head = grad_head + grad_head_inner
    returned_rim = shifted(grad_ext[None, :rim_rows].astype(jnp.bfloat16), "ctx", -1).astype(
        jnp.float32
    )
    own_rows = grad_ext[rim_rows:]
    own_rows = jnp.concatenate(
        [own_rows[: row_count - rim_rows], own_rows[row_count - rim_rows :] + returned_rim[0]],
        axis=0,
    )
    total_conv, total_head = lax.psum((grad_conv, grad_head), ("ctx", "fsdp"))
    return (own_rows[None].astype(jnp.bfloat16), grad_dt[None], total_conv, total_head)


def solution(mesh):
    return jax.shard_map(
        shards,
        mesh=mesh,
        in_specs=(P("fsdp", "ctx", None), P("fsdp", None, "ctx"), P("fsdp", "ctx", None), P(), P()),
        out_specs=(P("fsdp", "ctx", None), P("fsdp", None, "ctx"), P(), P()),
        check_vma=False,
    )
```

profile of v0, /device:TPU:25, one launch (start us, length us, event | category | flops | bytes accessed | tf_op | source)
XLA Modules:
  0.0 547.8 jit_solution(5632665170448419959)
XLA Ops:
  15.6 4.3 copy.69
  28.6 12.4 %fusion.11 = (f32[128,9216]{0,1:T(8,128)S(1)}, f32[128,9216]{0,1:T(8,128)}) fusion(f32[131,9216]{0,1:T(8,128)S(1)} %maximum_convert_fusion, f32[9216]{0:T(1024)S(1)} %bitcast.354, f32[9216]{0:T(1024)S(1)} %bitcast.356, f32[9216]{0:T(1024)S(1)} %bitcast.358, f32[9216]{0:T(1024)S(1)} %bitcast.352, f32[9216]{0:T(1024)S(1)} %bitcast.365), kind=kLoop, calls=%fused_computation.34 | loop fusion | flops 14155776 | bytes 28495872 | tf_op jit(solution)/shard_map/jvp(jit(silu))/mul | solution.py:61
  43.2 5.0 fusion.53
  48.3 7.5 %all-gather.1 = bf16[8,1,128]{2,1,0:T(2,128)(2,1)S(1)} all-gather(bf16[1,1,128]{2,1,0:T(2,128)(2,1)S(1)} %convert_bitcast_fusion.1), channel_id=2, replica_groups=mesh['ctx'=8,'fsdp'=4] {'ctx'}, dimensions={0}, use_global_device_ids=true | all-gather | bytes 2304 | tf_op jit(solution)/shard_map/all_gather | solution.py:28
  57.7 8.2 %fusion.1 = f32[4,32,128,64]{2,3,1,0:T(8,128)} fusion(bf16[4,32,64,128]{3,2,1,0:T(8,128)(2,1)S(1)} %bitcast.325, f32[4,128,128]{2,1,0:T(8,128)S(1)} %fusion.120, f32[4,32,128]{2,1,0:T(8,128)S(1)} %bitcast.371, f32[4,32,128]{2,1,0:T(8,128)S(1)} %bitcast.373, pred[128,128]{1,0:T(8,128)(4,1)S(1)} %iota_compare_fusion), kind=kOutput, calls=%fused_computation.9 | convolution fusion | flops 1623195648 | bytes 6701056 | tf_op jit(solution)/shard_map/transpose(jvp())/while/body/eval_jaxpr/gkts,sgkp->tgkp/dot_general | solution.py:91
  65.9 72.3 %all-gather.7.cloned.1.call-done = bf16[8,128,64,128]{3,2,1,0:T(8,128)(2,1)} async-done(((bf16[1,128,64,128]{3,2,1,0:T(8,128)(2,1)}), bf16[8,128,64,128]{3,2,1,0:T(8,128)(2,1)}) %all-gather.7.cloned.1.call-update) | async-done | bytes 16777232 | tf_op jit(solution)/shard_map/all_gather | solution.py:28
  140.8 32.8 %while.21 = (s32[]{:T(128)}, f32[128,64,128]{2,1,0:T(8,128)}, s32[]{:T(128)}, bf16[8,128]{1,0:T(8,128)(2,1)S(1)}, bf16[8,128,64,128]{3,2,1,0:T(8,128)(2,1)}, /*index=5*/s32[]{:T(128)}, s32[]{:T(128)}, s32[]{:T(128)}, s32[]{:T(128)}) while((s32[]{:T(128)}, f32[128,64,128]{2,1,0:T(8,128)}, s32[]{:T(128)}, bf16[8,128]{1,0:T(8,128)(2,1)S(1)}, ...), condition=%wide.region_7.8_spmd, body=%wide.region_6.7_spmd.sunk | while | flops 3145862 | bytes 10487195 | solution.py:43
  140.8 5.4 convert_add_fusion.6
  146.3 5.4 convert_add_fusion.6
  151.7 5.4 convert_add_fusion.6
  157.2 5.4 convert_add_fusion.6
  162.6 5.4 convert_add_fusion.6
  168.0 5.4 convert_add_fusion.6
  173.7 5.5 fusion.121
  179.2 8.7 %fusion.23 = (f32[128,4,32]{0,2,1:T(8,128)S(1)}, f32[128,4,32]{0,2,1:T(8,128)S(1)}, f32[4,32,64,128]{3,2,1,0:T(8,128)}) fusion(f32[128,9216]{0,1:T(8,128)} %copy-done.5, f32[4,32,64,128]{3,2,1,0:T(8,128)S(1)} %fusion.121, f32[128,4,128,1]{0,2,3,1:T(8,128)S(1)} %bitcast.336), kind=kOutput, calls=%fused_computation.50 | convolution fusion | flops 1614774272 | bytes 12976128 | tf_op jit(solution)/shard_map/transpose(jvp())/while/body/eval_jaxpr/sgkp,sgn->gkpn/dot_general | solution.py:102
  189.0 9.4 %fusion.16 = (f32[8192]{0:T(1024)}, f32[128,8192]{0,1:T(8,128)S(1)}, f32[128,8192]{0,1:T(8,128)}) fusion(bf16[1,128,8192]{1,2,0:T(8,128)(2,1)S(1)} %copy.65, f32[128,9216]{0,1:T(8,128)} %copy-done.5, f32[4,32,64,128]{3,2,1,0:T(8,128)} %copy-done.6, f32[128,128]{0,1:T(8,128)S(1)} %copy.73, f32[4,32,128,64]{2,3,1,0:T(8,128)} %fusion.1, ...), kind=kLoop, calls=%fused_computation.39 | loop fusion | flops 9428992 | bytes 27459584 | tf_op jit(solution)/shard_map/transpose(jvp())/reduce_sum | solution.py:110
  200.2 4.9 fusion.50
  210.1 13.2 %fusion.37 = (f32[4,32,128]{2,1,0:T(8,128)}, f32[4,32,128]{2,1,0:T(8,128)}, f32[4,32,128]{2,1,0:T(8,128)}, f32[4,128,128]{2,1,0:T(8,128)S(1)}) fusion(f32[4,32,128]{2,1,0:T(8,128)S(1)} %bitcast.372, f32[4,32,128]{2,1,0:T(8,128)} %bitcast.374, f32[4,128,128]{2,1,0:T(8,128)} %copy-done.13, pred[128,128]{1,0:T(8,128)(4,1)} %copy-done.20, ...), kind=kOutput, calls=%fused_computation.65 | convolution fusion | flops 1646149632 | bytes 7159808 | tf_op jit(solution)/shard_map/transpose(jvp())/while/body/eval_jaxpr/gkts,sgkp->tgkp/dot_general | solution.py:91
  238.7 5.9 %fusion.68 = f32[128,4,128]{0,2,1:T(8,128)S(1)} fusion(f32[128,4,32,64]{0,3,2,1:T(8,128)} %bitcast.322, f32[128,4,32]{0,2,1:T(8,128)S(1)} %bitcast.351), kind=kOutput, calls=%fused_computation.95 | convolution fusion | flops 1611661312 | bytes 4521984 | tf_op jit(solution)/shard_map/transpose(jvp())/while/body/eval_jaxpr/sgkp,sgn->gkpn/dot_general | solution.py:102
  244.6 9.1 %fusion.54 = f32[128,4,128]{0,2,1:T(8,128)S(1)} fusion(f32[4,32,64,128]{3,2,1,0:T(8,128)S(1)} %bitcast.317, f32[128,4,32,64]{0,3,2,1:T(8,128)} %bitcast.323, f32[128,4,32]{0,2,1:T(8,128)S(1)} %bitcast.346), kind=kOutput, calls=%fused_computation.87 | convolution fusion | flops 1611661312 | bytes 8716288 | tf_op jit(solution)/shard_map/transpose(jvp(sgkp,sgn->gkpn))/dot_general | solution.py:120
  254.1 45.6 %all-gather.5.cloned.1.call-done = bf16[8,128,64,128]{3,2,1,0:T(8,128)(2,1)} async-done(((bf16[1,128,64,128]{3,2,1,0:T(8,128)(2,1)}), bf16[8,128,64,128]{3,2,1,0:T(8,128)(2,1)}) %all-gather.5.cloned.1.call-update) | async-done | bytes 16777232 | tf_op jit(solution)/shard_map/all_gather | solution.py:28
  302.2 6.0 %while.20 = (s32[]{:T(128)}, f32[128,64,128]{2,1,0:T(8,128)}, s32[]{:T(128)}, bf16[8,128]{1,0:T(8,128)(2,1)}, bf16[8,128,64,128]{3,2,1,0:T(8,128)(2,1)}, /*index=5*/s32[]{:T(128)}, s32[]{:T(128)}, s32[]{:T(128)}) while((s32[]{:T(128)}, f32[128,64,128]{2,1,0:T(8,128)}, s32[]{:T(128)}, bf16[8,128]{1,0:T(8,128)(2,1)}, ...), condition=%wide.region_5.6_spmd, body=%wide.region_4.5_spmd.sunk | while | flops 3145861 | bytes 10487175 | solution.py:43
  302.8 5.3 convert_add_fusion.5
  308.1 9.9 %fusion.57 = f32[4,128,128]{1,2,0:T(8,128)} fusion(f32[4,32,64,128]{3,2,1,0:T(8,128)} %bitcast.318, bf16[128,4,32,64]{0,3,2,1:T(8,128)(2,1)S(1)} %bitcast.328, f32[128,4,32]{0,2,1:T(8,128)S(1)} %bitcast.350), kind=kOutput, calls=%fused_computation.88 | convolution fusion | flops 1612709888 | bytes 6619136 | tf_op jit(solution)/shard_map/transpose(jvp(tgn,gkpn->tgkp))/dot_general | solution.py:128
  318.1 4.2 fusion.20
  328.6 4.6 fusion.63
  334.8 21.0 %multiply_reduce_fusion.4 = (f32[9216]{0:T(1024)S(1)}, f32[9216]{0:T(1024)S(1)}, f32[9216]{0:T(1024)S(1)}, f32[9216]{0:T(1024)S(1)}, f32[9216]{0:T(1024)S(1)}, /*index=5*/f32[128,9216]{0,1:T(8,128)S(1)}) fusion(f32[131,9216]{0,1:T(8,128)} %copy-done.3, f32[128,9216]{0,1:T(8,128)} %get-tuple-element.537, f32[128,8192]{0,1:T(8,128)} %get-tuple-element.546, ...), kind=kLoop, calls=%fused_computation.32 | loop fusion | flops 23546880 | bytes 33214464 | tf_op jit(solution)/shard_map/transpose(jvp())/reduce_sum | solution.py:60
  355.9 6.1 %broadcast_multiply_fusion.3 = (f32[128,9216]{0,1:T(8,128)S(1)}, f32[128,9216]{0,1:T(8,128)S(1)}, f32[128,9216]{0,1:T(8,128)S(1)}, f32[128,9216]{0,1:T(8,128)S(1)}) fusion(f32[128,9216]{0,1:T(8,128)S(1)} %get-tuple-element.531, f32[9216]{0:T(1024)S(1)} %bitcast.355, f32[9216]{0:T(1024)S(1)} %bitcast.353, f32[9216]{0:T(1024)S(1)} %bitcast.359, ...), kind=kLoop, calls=%fused_computation.73 | loop fusion | flops 4718592 | bytes 23740416 | tf_op jit(solution)/shard_map/transpose(jvp())/mul | solution.py:60
  362.0 9.4 %fusion.117 = (bf16[131,9216]{0,1:T(8,128)(2,1)S(1)}, f32[131,9216]{0,1:T(8,128)}) fusion(f32[128,9216]{0,1:T(8,128)S(1)} %get-tuple-element.541, f32[128,9216]{0,1:T(8,128)S(1)} %get-tuple-element.542, f32[128,9216]{0,1:T(8,128)S(1)} %get-tuple-element.543, f32[128,9216]{0,1:T(8,128)S(1)} %get-tuple-element.540), kind=kLoop, calls=%fused_computation.175 | loop fusion | flops 4829184 | bytes 26118144 | tf_op jit(solution)/shard_map/convert.12
  380.1 71.3 %psum.15 = f32[3,128]{1,0:T(4,128)} all-reduce(f32[3,128]{1,0:T(4,128)S(1)} %pad_add_fusion.3), channel_id=1, replica_groups=mesh['ctx'=8,'fsdp'=4] {'ctx','fsdp'}, use_global_device_ids=true, to_apply=%region_31.32 | all-reduce | flops 384 | bytes 3072 | tf_op jit(solution)/shard_map/psum | solution.py:200
  459.1 4.3 copy.95
  463.3 75.8 %all-reduce.21.cloned.1.call-done = f32[5,9216]{1,0:T(8,128)} async-done(((f32[5,9216]{1,0:T(8,128)}), f32[5,9216]{1,0:T(8,128)}) %all-reduce.21.cloned.1.call-update) | async-done | bytes 184336 | tf_op jit(solution)/shard_map/psum | solution.py:200
  (133 shorter events, 76.5 us)
Async XLA Ops:
  7.2 131.1 %all-gather.7.cloned.1.call-start = ((), (), s32[]{:S(2)}) async-start(), calls=%async_computation.1 | async-start | bytes 18874368 | tf_op jit(solution)/shard_map/all_gather | solution.py:28
  8.2 15.0 %collective-permute-start = (bf16[1,3,9216]{2,1,0:T(4,128)(2,1)S(1)}, bf16[1,3,9216]{2,1,0:T(4,128)(2,1)S(1)}, u32[]{:S(2)}, u32[]{:S(2)}) collective-permute-start(bf16[1,3,9216]{2,1,0:T(4,128)(2,1)S(1)} %slice.83), channel_id=1, source_target_pairs={{0,4},{4,8},{8,12},{12,16},{16,20},{20,24},{24,28},{1,5},{5,9},{9,... | collective-permute-start | bytes 165896 | tf_op jit(solution)/shard_map/ppermute | solution.py:20
  13.6 15.0 %copy-start.7 = (f32[1,9216]{1,0:T(1,128)}, f32[1,9216]{1,0:T(1,128)S(1)}, u32[]{:S(2)}) copy-start(f32[1,9216]{1,0:T(1,128)S(1)} %get-tuple-element.549) | copy-start | bytes 110596
  13.6 15.0 %copy-start.9 = (f32[1,9216]{1,0:T(1,128)}, f32[1,9216]{1,0:T(1,128)S(1)}, u32[]{:S(2)}) copy-start(f32[1,9216]{1,0:T(1,128)S(1)} %get-tuple-element.550) | copy-start | bytes 110596
  13.6 15.0 %copy-start.11 = (f32[1,9216]{1,0:T(1,128)}, f32[1,9216]{1,0:T(1,128)S(1)}, u32[]{:S(2)}) copy-start(f32[1,9216]{1,0:T(1,128)S(1)} %get-tuple-element.551) | copy-start | bytes 110596
  28.6 12.4 %copy-start.3 = (f32[131,9216]{0,1:T(8,128)}, f32[131,9216]{0,1:T(8,128)S(1)}, u32[]{:S(2)}) copy-start(f32[131,9216]{0,1:T(8,128)S(1)} %maximum_convert_fusion) | copy-start | bytes 14487556
  41.0 2.1 copy-start.5
  48.2 251.5 %all-gather.5.cloned.1.call-start = ((), (), s32[]{:S(2)}) async-start(), calls=%async_computation | async-start | bytes 18874368 | tf_op jit(solution)/shard_map/all_gather | solution.py:28
  56.1 9.8 %copy-start.17 = (f32[128,128]{1,0:T(8,128)}, f32[128,128]{1,0:T(8,128)S(1)}, u32[]{:S(2)}) copy-start(f32[128,128]{1,0:T(8,128)S(1)} %copy.71) | copy-start | bytes 196612
  56.2 9.7 %copy-start.19 = (f32[1,128,128]{2,1,0:T(8,128)}, f32[1,128,128]{2,1,0:T(8,128)S(1)}, u32[]{:S(2)}) copy-start(f32[1,128,128]{2,1,0:T(8,128)S(1)} %copy.70) | copy-start | bytes 196612
  56.4 9.5 %copy-start.20 = (pred[128,128]{1,0:T(8,128)(4,1)}, pred[128,128]{1,0:T(8,128)(4,1)S(1)}, u32[]{:S(2)}) copy-start(pred[128,128]{1,0:T(8,128)(4,1)S(1)} %iota_compare_fusion) | copy-start | bytes 49156
  56.4 131.6 %copy-start.24 = (f32[128]{0:T(128)}, f32[128]{0:T(128)S(1)}, u32[]{:S(2)}) copy-start(f32[128]{0:T(128)S(1)} %slice_bitcast_fusion.5) | copy-start | bytes 1540
  57.6 8.2 %copy-start.13 = (f32[4,128,128]{2,1,0:T(8,128)}, f32[4,128,128]{2,1,0:T(8,128)S(1)}, u32[]{:S(2)}) copy-start(f32[4,128,128]{2,1,0:T(8,128)S(1)} %fusion.120) | copy-start | bytes 786436
  173.7 5.5 %copy-start.22 = (bf16[8,128]{1,0:T(8,128)(2,1)}, bf16[8,128]{1,0:T(8,128)(2,1)S(1)}, u32[]{:S(2)}) copy-start(bf16[8,128]{1,0:T(8,128)(2,1)S(1)} %get-tuple-element.706) | copy-start | bytes 6148
  179.2 8.7 %copy-start.6 = (f32[4,32,64,128]{3,2,1,0:T(8,128)}, f32[4,32,64,128]{3,2,1,0:T(8,128)S(1)}, u32[]{:S(2)}) copy-start(f32[4,32,64,128]{3,2,1,0:T(8,128)S(1)} %fusion.121) | copy-start | bytes 12582916
  198.3 1.9 copy-start.4
  205.1 5.0 copy-start.18
  205.2 334.0 %all-reduce.21.cloned.1.call-start = ((), (), s32[]{:S(2)}) async-start(), calls=%async_computation.2 | async-start | bytes 589824 | tf_op jit(solution)/shard_map/psum | solution.py:200
  238.7 5.9 %copy-start = (f32[128,64,128]{2,1,0:T(8,128)S(1)}, f32[128,64,128]{2,1,0:T(8,128)}, u32[]{:S(2)}) copy-start(f32[128,64,128]{2,1,0:T(8,128)} %get-tuple-element.485) | copy-start | bytes 12582916
  308.1 9.9 %copy-start.2 = (f32[128,64,128]{2,1,0:T(8,128)S(1)}, f32[128,64,128]{2,1,0:T(8,128)}, u32[]{:S(2)}) copy-start(f32[128,64,128]{2,1,0:T(8,128)} %get-tuple-element.484) | copy-start | bytes 12582916
  318.1 4.2 copy-start.1
  322.3 3.5 copy-start.14
  322.3 3.5 copy-start.15
  322.3 3.5 copy-start.16
  334.8 21.1 %copy-start.8 = (f32[1,9216]{1,0:T(1,128)S(1)}, f32[1,9216]{1,0:T(1,128)}, u32[]{:S(2)}) copy-start(f32[1,9216]{1,0:T(1,128)} %copy-done.7) | copy-start | bytes 110596
  334.8 21.1 %copy-start.10 = (f32[1,9216]{1,0:T(1,128)S(1)}, f32[1,9216]{1,0:T(1,128)}, u32[]{:S(2)}) copy-start(f32[1,9216]{1,0:T(1,128)} %copy-done.9) | copy-start | bytes 110596
  334.8 21.1 %copy-start.12 = (f32[1,9216]{1,0:T(1,128)S(1)}, f32[1,9216]{1,0:T(1,128)}, u32[]{:S(2)}) copy-start(f32[1,9216]{1,0:T(1,128)} %copy-done.11) | copy-start | bytes 110596
  372.9 6.5 %copy-start.25 = (f32[128]{0:T(128)S(1)}, f32[128]{0:T(128)}, u32[]{:S(2)}) copy-start(f32[128]{0:T(128)} %get-tuple-element.552) | copy-start | bytes 1540
  372.9 7.2 %copy-start.21 = (f32[128]{0:T(128)S(1)}, f32[128]{0:T(128)}, u32[]{:S(2)}) copy-start(f32[128]{0:T(128)} %reduce_sum.319) | copy-start | bytes 1540
  372.9 7.2 %copy-start.23 = (f32[128]{0:T(128)S(1)}, f32[128]{0:T(128)}, u32[]{:S(2)}) copy-start(f32[128]{0:T(128)} %get-tuple-element.529) | copy-start | bytes 1540
  375.8 75.6 %collective-permute-start.1 = (bf16[1,3,9216]{2,1,0:T(4,128)(2,1)S(1)}, bf16[1,3,9216]{2,1,0:T(4,128)(2,1)S(1)}, u32[]{:S(2)}, u32[]{:S(2)}) collective-permute-start(bf16[1,3,9216]{2,1,0:T(4,128)(2,1)S(1)} %copy.84), channel_id=1, source_target_pairs={{4,0},{8,4},{12,8},{16,12},{20,16},{24,20},{28,24},{5,1},{9,5},{13... | collective-permute-start | bytes 165896 | tf_op jit(solution)/shard_map/ppermute | solution.py:20
Sparse Core Ops, SparseCore 0:
  48.4 89.8 all-gather.6
  205.3 94.3 all-gather.4
  379.5 159.6 all-reduce.20
where the time goes:
time: 558 us; the launch traced here: 548 us
  waiting for transfers between devices  194 us (35%)
  other arithmetic  125 us (22%)
  matrix products  85.6 us (15%)
  blocking collectives  78.8 us (14%)
  local copies, waits for them, and re-layouts  43.4 us (8%)
  between operations  14.8 us (3%)
  starting transfers between devices  6.13 us (1%)
    all_gather x2, waiting for transfers between devices, entering_2(): lax.all_gather(a.astype(kind), axis)  118 us
    psum x1, waiting for transfers between devices, shards(): total_conv, total_head = lax.psum((grad_conv, grad_head), ('ctx', 'fsdp'))  75.8 us
    psum x1, blocking collectives, shards(): total_conv, total_head = lax.psum((grad_conv, grad_head), ('ctx', 'fsdp'))  71.3 us
    add x7, other arithmetic, combine_carry(): later_pair[0][:, None, None] * earlier_pair[1] + later_pair[1]  37.9 us
    dot_general x2, matrix products, advance(): jnp.einsum('gkts,sgkp->tgkp', weights, x_grouped, precision=exact_prec)  21.4 us
    reduce_sum x1, other arithmetic, prepare(): conv_params[offset][None, :] * extended[offset:offset + row_count]  21 us
    dot_general x3, matrix products, end_state(): jnp.einsum('sgkp,sgn->gkpn', weighted, b_groups, precision=exact_prec)  19.4 us
    unnamed x59, local copies, waits for them, and re-layouts  19.2 us
  transfers between devices with their start and end apart: 5, of which 3 were waited for; matrix products, arithmetic and copies ran while one was open for 15% of the time, Pallas kernels for 0%

commit v1 on v0

v1 whole, which is shorter than its diff:
```python
import functools

import jax
import jax.numpy as jnp
from jax import lax
from jax.experimental import pallas as pl
from jax.experimental.pallas import tpu as pltpu
from jax.sharding import PartitionSpec as P

HEADS = 128
HEAD_DIM = 64
STATE = 128
GROUPS = 4
CONV_W = 4
T = 128
LANES = 128
X_WIDTH = HEADS * HEAD_DIM
CHANNELS = X_WIDTH + 2 * GROUPS * STATE
PAIRS = HEADS // 2
PER_GROUP = PAIRS // GROUPS
F32 = jnp.float32
BF16 = jnp.bfloat16
MESH = pl.DeviceIdType.MESH
CHUNKS = 16
CHUNK_HEADS = HEADS // CHUNKS
CHUNK_ROWS = X_WIDTH // CHUNKS
LAG = 2
TAIL = 16
BLOCKS = CHANNELS // LANES


def dot(a, b, ca, cb, precision=None):
    return lax.dot_general(
        a, b, (((ca,), (cb,)), ((), ())), precision=precision, preferred_element_type=F32
    )


def block_of(i):
    return pl.ds(pl.multiple_of(i * LANES, LANES), LANES)


def sigmoid(v):
    return 1.0 / (1.0 + jnp.exp(-v))


def softplus(v):
    z = jnp.exp(-jnp.abs(v))
    small = z * (1.0 - z * (0.5 - z * (1.0 / 3.0 - z * 0.25)))
    return jnp.maximum(v, 0.0) + jnp.where(z < 0.01, small, jnp.log(1.0 + z))


def iota2(shape, dim):
    return lax.broadcasted_iota(jnp.int32, shape, dim)


def wide_pair(ht_ref, h):
    top = jnp.broadcast_to(ht_ref[pl.ds(h, 1), :], (HEAD_DIM, T))
    low = jnp.broadcast_to(ht_ref[pl.ds(h + 1, 1), :], (HEAD_DIM, T))
    return jnp.concatenate([top, low], axis=0).T


def states_kernel(
    xbc_ref, halo_ref, dt_ref, dy_ref, conv_ref, head_ref,
    mixed_ref, leave_ref, pull_ref, fade_ref, run_ref, step_ref, b_ref, c_ref,
    ext,
):
    step_th = softplus(dt_ref[...].astype(F32).T + head_ref[0:1, :])
    rate_th = step_th * jnp.exp(head_ref[1:2, :])
    lower = (iota2((T, T), 0) >= iota2((T, T), 1)).astype(F32)
    run_ht = dot(lower, rate_th, 1, 0, lax.Precision.HIGHEST).T
    run_ref[...] = run_ht
    step_ref[...] = step_th.T
    fade_ref[...] = jnp.broadcast_to(jnp.exp(-run_ht[:, T - 1 : T]), (HEADS, LANES))

    def convolve(i):
        cols = block_of(i)
        ext[0:8, :] = halo_ref[:, cols].astype(F32)
        ext[8 : 8 + T, :] = xbc_ref[:, cols].astype(F32)
        mixed = conv_ref[CONV_W : CONV_W + 1, cols] + conv_ref[0:1, cols] * ext[5 : 5 + T, :]
        for j in range(1, CONV_W):
            mixed = mixed + conv_ref[j : j + 1, cols] * ext[5 + j : 5 + j + T, :]
        mixed_ref[:, cols] = mixed
        return mixed * sigmoid(mixed)

    def bc(g, _):
        b_ref[:, block_of(g)] = convolve(PAIRS + g).astype(BF16)
        c_ref[:, block_of(g)] = convolve(PAIRS + GROUPS + g).astype(BF16)
        return 0

    lax.fori_loop(0, GROUPS, bc, 0)

    def pair(i, _):
        g = i // PER_GROUP
        x = convolve(i)
        run = wide_pair(run_ref, 2 * i)
        step = wide_pair(step_ref, 2 * i)
        tail = (x * step * jnp.exp(run - run[T - 1 : T, :])).astype(BF16)
        out = (jnp.exp(-run) * dy_ref[:, block_of(i)].astype(F32)).astype(BF16)
        leave_ref[block_of(i), :] = dot(tail, b_ref[:, block_of(g)], 0, 0)
        pull_ref[block_of(i), :] = dot(out, c_ref[:, block_of(g)], 0, 0)
        return 0

    lax.fori_loop(0, PAIRS, pair, 0)


def chain_kernel(count, leave_ref, pull_ref, fade_ref, enter_ref, later_ref,
                 out_f, out_b, in_f, in_b, send_f, recv_f, send_b, recv_b):
    me = lax.axis_index("ctx")
    barrier = pltpu.get_barrier_semaphore()
    first, last = me == 0, me == count - 1

    for peer in (lax.rem(me + 1, count), lax.rem(me + count - 1, count)):
        pl.semaphore_signal(barrier, inc=1, device_id={"ctx": peer}, device_id_type=MESH)
    pl.semaphore_wait(barrier, 2)

    def rows_of(c):
        return pl.ds(pl.multiple_of(c * CHUNK_ROWS, CHUNK_ROWS), CHUNK_ROWS)

    def copy(c, src, dst, send, recv, peer):
        return pltpu.make_async_remote_copy(
            src_ref=src.at[rows_of(c)], dst_ref=dst.at[rows_of(c)],
            send_sem=send.at[c], recv_sem=recv.at[c],
            device_id={"ctx": peer}, device_id_type=MESH,
        )

    def handle(c, own, src, dst, send, recv, peer, begins, ends, result):
        @pl.when(begins)
        def _():
            result[rows_of(c), :] = jnp.zeros((CHUNK_ROWS, LANES), BF16)

        @pl.when(jnp.logical_not(begins))
        def _():
            copy(c, src, dst, send, recv, peer).wait_recv()
            result[rows_of(c), :] = dst[rows_of(c), :]

        @pl.when(jnp.logical_not(ends))
        def _():
            for k in range(CHUNK_HEADS):
                rows = pl.ds(pl.multiple_of(c * CHUNK_ROWS + k * HEAD_DIM, HEAD_DIM), HEAD_DIM)
                fade = fade_ref[pl.ds(c * CHUNK_HEADS + k, 1), :]
                src[rows, :] = (fade * result[rows, :].astype(F32) + own[rows, :]).astype(BF16)
            copy(c, src, dst, send, recv, peer).start()

    up = jnp.minimum(me + 1, count - 1)
    down = jnp.maximum(me - 1, 0)

    def tick(v, _):
        c = v - me * LAG

        @pl.when(jnp.logical_and(c >= 0, c < CHUNKS))
        def _():
            handle(c, leave_ref, out_f, in_f, send_f, recv_f, up, first, last, enter_ref)

        d = v - (count - 1 - me) * LAG

        @pl.when(jnp.logical_and(d >= 0, d < CHUNKS))
        def _():
            handle(d, pull_ref, out_b, in_b, send_b, recv_b, down, last, first, later_ref)

        return 0

    lax.fori_loop(0, CHUNKS + (count - 1) * LAG, tick, 0)

    def drain(c, _):
        @pl.when(jnp.logical_not(last))
        def _():
            copy(c, out_f, in_f, send_f, recv_f, up).wait_send()

        @pl.when(jnp.logical_not(first))
        def _():
            copy(c, out_b, in_b, send_b, recv_b, down).wait_send()

        return 0

    lax.fori_loop(0, CHUNKS, drain, 0)


def grads_kernel(
    xbc_ref, halo_ref, dt_ref, dy_ref, conv_ref, head_ref,
    mixed_ref, run_ref, step_ref, b_ref, c_ref, enter_ref, later_ref,
    dx_ref, tail_ref, rim_ref, packed_ref, ddt_ref,
    ext, dms, skip_ref, scores, dscores, db, dc, acc,
):
    skip_ref[...] = jnp.broadcast_to(head_ref[2:3, :], (LANES, HEADS)).T
    acc[...] = jnp.zeros_like(acc)
    packed_ref[...] = jnp.zeros_like(packed_ref)
    dms[0:8, :] = jnp.zeros((8, LANES), F32)
    dms[8 + T : 16 + T, :] = jnp.zeros((8, LANES), F32)
    causal = iota2((T, T), 0) >= iota2((T, T), 1)
    lane = iota2((T, LANES), 1)
    left = lane < HEAD_DIM

    def conv_back(i, mixed, sig, dact):
        cols = block_of(i)
        dm = dact * (sig * (1.0 + mixed * (1.0 - sig)))
        dms[8 : 8 + T, :] = dm
        ext[0:8, :] = halo_ref[:, cols].astype(F32)
        ext[8 : 8 + T, :] = xbc_ref[:, cols].astype(F32)
        taps = [conv_ref[j : j + 1, cols] for j in range(CONV_W)]
        own = taps[3] * dm
        rim = taps[0] * dms[8:16, :]
        for j in range(3):
            own = own + taps[j] * dms[11 - j : 11 - j + T, :]
        for j in range(1, 3):
            rim = rim + taps[j] * dms[8 - j : 16 - j, :]
        dx_ref[:, cols] = own.astype(BF16)
        tail_ref[:, cols] = own[T - TAIL :, :]
        rim_ref[:, cols] = jnp.concatenate([rim, jnp.zeros_like(rim)], 0).astype(BF16)
        for j in range(CONV_W):
            packed_ref[i, j : j + 1, :] = jnp.sum(dm * ext[5 + j : 5 + j + T, :], 0, keepdims=True)
        packed_ref[i, CONV_W : CONV_W + 1, :] = jnp.sum(dm, 0, keepdims=True)

    def pair(i, g):
        h = 2 * i
        cols = block_of(i)
        mixed = mixed_ref[:, cols]
        sig = sigmoid(mixed)
        x = mixed * sig
        dy16 = dy_ref[:, cols]
        dy = dy16.astype(F32)
        step = wide_pair(step_ref, h)
        fades = []
        runs = []
        for k in range(2):
            row = jnp.broadcast_to(run_ref[pl.ds(h + k, 1), :], (T, T))
            col = row.T
            runs.append(col)
            fades.append(jnp.exp(jnp.where(causal, row - col, -1e30)))
        run = jnp.where(left, runs[0], runs[1])
        xd16 = (x * step).astype(BF16)
        xd = xd16.astype(F32)
        e_tail = jnp.exp(run - run[T - 1 : T, :])
        e_head = jnp.exp(-run)
        zero = jnp.zeros((T, LANES), BF16)
        bd_x = jnp.concatenate([jnp.where(left, xd16, zero), jnp.where(left, zero, xd16)], 0)
        bd_y = jnp.concatenate([jnp.where(left, dy16, zero), jnp.where(left, zero, dy16)], 0)
        sc = scores[...]
        w = [(sc * f).astype(BF16) for f in fades]
        enter = enter_ref[cols, :]
        later = later_ref[cols, :]
        b16 = b_ref[:, block_of(g)]
        c16 = c_ref[:, block_of(g)]
        y = dot(jnp.concatenate(w, 1), bd_x, 1, 0) + e_head * dot(c16, enter, 1, 1)
        from_tail = e_tail * dot(b16, later, 1, 1)
        dxd = dot(jnp.concatenate(w, 0), bd_y, 0, 0) + from_tail
        pairwise = dot(dy16, bd_x, 1, 1)
        dscores[...] += pairwise[:, :T] * fades[0] + pairwise[:, T:] * fades[1]
        dc[...] += dot((e_head * dy).astype(BF16), enter, 1, 0)
        db[...] += dot((xd * e_tail).astype(BF16), later, 1, 0)
        skip = jnp.where(left[0:1, :], skip_ref[pl.ds(h, 1), :], skip_ref[pl.ds(h + 1, 1), :])
        conv_back(i, mixed, sig, step * dxd + skip * dy)
        both = (enter.astype(F32) * later.astype(F32)).astype(BF16)
        passed = dot(jnp.ones((8, STATE), BF16), both, 1, 1)
        sub = iota2((8, LANES), 0)
        rows = jnp.where(sub == 0, jnp.sum(dy * x, 0, keepdims=True), 0.0)
        rows = rows + jnp.where(
            sub == 1,
            jnp.sum(xd * from_tail, 0, keepdims=True) + e_head[T - 1 : T, :] * passed[0:1, :],
            0.0,
        )
        value = jnp.concatenate([xd * dxd - dy * y, x * dxd, rows], 0)
        high = value.astype(BF16)
        low = (value - high.astype(F32)).astype(BF16)
        pick = (iota2((LANES, HEADS), 1) == h + iota2((LANES, HEADS), 0) // HEAD_DIM).astype(BF16)
        acc[...] += dot(
            jnp.concatenate([high, low], 1), jnp.concatenate([pick, pick], 0), 1, 0
        )

    def group(g, _):
        b16 = b_ref[:, block_of(g)]
        c16 = c_ref[:, block_of(g)]
        scores[...] = dot(c16, b16, 1, 1)
        dscores[...] = jnp.zeros_like(dscores)
        db[...] = jnp.zeros_like(db)
        dc[...] = jnp.zeros_like(dc)

        def inner(k, _):
            pair(g * PER_GROUP + k, g)
            return 0

        lax.fori_loop(0, PER_GROUP, inner, 0)
        ds = dscores[...].astype(BF16)
        for at, total in (
            (PAIRS + g, db[...] + dot(ds, c16, 0, 0)),
            (PAIRS + GROUPS + g, dc[...] + dot(ds, b16, 1, 0)),
        ):
            mixed = mixed_ref[:, block_of(at)]
            conv_back(at, mixed, sigmoid(mixed), total)
        return 0

    lax.fori_loop(0, GROUPS, group, 0)

    upper = (iota2((T, T), 0) <= iota2((T, T), 1)).astype(F32)
    d_rate = dot(upper, acc[0:T, :], 1, 0, lax.Precision.HIGHEST) - acc[2 * T + 1 : 2 * T + 2, :]
    scale = jnp.exp(head_ref[1:2, :])
    raw = dt_ref[...].astype(F32).T + head_ref[0:1, :]
    d_dt = (acc[T : 2 * T, :] + d_rate * scale) * sigmoid(raw)
    ddt_ref[...] = d_dt.T
    packed_ref[BLOCKS, 0:1, :] = jnp.sum(d_dt, 0, keepdims=True)
    packed_ref[BLOCKS, 1:2, :] = jnp.sum(d_rate * softplus(raw) * scale, 0, keepdims=True)
    packed_ref[BLOCKS, 2:3, :] = acc[2 * T : 2 * T + 1, :]


def sum_kernel(
    counts, packed_ref, tail_ref, rim_ref, conv_ref, head_ref, end_ref,
    parts, mine, planes, total, rim_in, send_a, recv_a, send_b, recv_b, send_c, recv_c, rim_sem,
):
    n, m = counts
    share = packed_ref.shape[0] // n
    me, plane = lax.axis_index("ctx"), lax.axis_index("fsdp")
    barrier = pltpu.get_barrier_semaphore()
    for r in range(1, n):
        peer = lax.rem(me + r, n)
        pl.semaphore_signal(barrier, inc=1, device_id={"ctx": peer}, device_id_type=MESH)
    for r in range(1, m):
        peer = lax.rem(plane + r, m)
        pl.semaphore_signal(barrier, inc=1, device_id={"fsdp": peer}, device_id_type=MESH)
    pl.semaphore_wait(barrier, n + m - 2)

    def piece(k):
        return pl.ds(k * share, share)

    def rim_copy():
        return pltpu.make_async_remote_copy(
            src_ref=rim_ref, dst_ref=rim_in, send_sem=rim_sem.at[0], recv_sem=rim_sem.at[1],
            device_id={"ctx": jnp.maximum(me - 1, 0)}, device_id_type=MESH,
        )

    def scatter(peer, slot):
        return pltpu.make_async_remote_copy(
            src_ref=packed_ref.at[piece(peer)], dst_ref=parts.at[slot],
            send_sem=send_a.at[peer], recv_sem=recv_a.at[slot],
            device_id={"ctx": peer}, device_id_type=MESH,
        )

    def across(peer, slot):
        return pltpu.make_async_remote_copy(
            src_ref=mine, dst_ref=planes.at[slot],
            send_sem=send_b.at[peer], recv_sem=recv_b.at[slot],
            device_id={"fsdp": peer}, device_id_type=MESH,
        )

    def gather(peer, slot):
        return pltpu.make_async_remote_copy(
            src_ref=total.at[piece(me)], dst_ref=total.at[piece(slot)],
            send_sem=send_c.at[peer], recv_sem=recv_c.at[slot],
            device_id={"ctx": peer}, device_id_type=MESH,
        )

    for r in range(1, n):
        scatter(lax.rem(me + r, n), me).start()

    @pl.when(me > 0)
    def _():
        rim_copy().start()

    parts[me] = packed_ref[piece(me)]
    for r in range(1, n):
        scatter(me, lax.rem(me + r, n)).wait_recv()
    own = parts[0]
    for k in range(1, n):
        own = own + parts[k]
    mine[...] = own
    for r in range(1, m):
        across(lax.rem(plane + r, m), plane).start()
    planes[plane] = own
    for r in range(1, m):
        across(plane, lax.rem(plane + r, m)).wait_recv()
    own = planes[0]
    for k in range(1, m):
        own = own + planes[k]
    total[piece(me)] = own
    for r in range(1, n):
        gather(lax.rem(me + r, n), me).start()

    @pl.when(me == n - 1)
    def _():
        end_ref[...] = tail_ref[...].astype(BF16)

    @pl.when(me < n - 1)
    def _():
        rim_copy().wait_recv()
        shift = TAIL - (CONV_W - 1)
        back = rim_in[...].astype(F32)
        pad = jnp.zeros((shift, CHANNELS), F32)
        moved = jnp.concatenate([pad, back[0 : CONV_W - 1, :]], 0)
        end_ref[...] = (tail_ref[...] + moved).astype(BF16)

    for r in range(1, n):
        gather(me, lax.rem(me + r, n)).wait_recv()
    for i in range(BLOCKS):
        conv_ref[:, i * LANES : (i + 1) * LANES] = total[i, 0 : CONV_W + 1, :]
    head_ref[...] = total[BLOCKS, 0:3, :]
    for r in range(1, n):
        scatter(lax.rem(me + r, n), me).wait_send()
        gather(lax.rem(me + r, n), me).wait_send()
    for r in range(1, m):
        across(lax.rem(plane + r, m), plane).wait_send()

    @pl.when(me > 0)
    def _():
        rim_copy().wait_send()


def vmem(count):
    return [pl.BlockSpec(memory_space=pltpu.VMEM)] * count


def call(kernel, out, scratch, args, limit=56, **params):
    return pl.pallas_call(
        kernel,
        out_shape=[jax.ShapeDtypeStruct(s, d) for s, d in out],
        in_specs=vmem(len(args)),
        out_specs=vmem(len(out)),
        scratch_shapes=scratch,
        compiler_params=pltpu.CompilerParams(vmem_limit_bytes=limit << 20, **params),
    )(*args)


def shifted(block, axis, distance):
    devices = range(lax.axis_size(axis))
    route = [(i - distance, i) for i in devices if i - distance in devices]
    return lax.ppermute(block, axis, route)


def shards(xbc, dt_raw, dy, conv_params, head_params):
    rim_rows = CONV_W - 1
    count = lax.axis_size("ctx")
    x = xbc[0]
    halo = jnp.pad(shifted(x[T - rim_rows :], "ctx", 1), ((8 - rim_rows, 0), (0, 0)))
    base = (x, halo, dt_raw[0], dy[0], conv_params, head_params)
    bc_width = GROUPS * STATE
    mixed, leave, pull, fade, run, step, b, c = call(
        states_kernel,
        [((T, CHANNELS), F32), ((X_WIDTH, STATE), F32), ((X_WIDTH, STATE), F32),
         ((HEADS, LANES), F32), ((HEADS, T), F32), ((HEADS, T), F32),
         ((T, bc_width), BF16), ((T, bc_width), BF16)],
        [pltpu.VMEM((8 + T, LANES), F32)],
        base,
    )
    wire = pltpu.VMEM((X_WIDTH, STATE), BF16)
    sems = pltpu.SemaphoreType.DMA((CHUNKS,))
    enter, later = call(
        functools.partial(chain_kernel, count),
        [((X_WIDTH, STATE), BF16)] * 2,
        [wire, wire, wire, wire, sems, sems, sems, sems],
        (leave, pull, fade),
        collective_id=0,
        has_side_effects=True,
    )
    planes = lax.axis_size("fsdp")
    share = pl.cdiv(BLOCKS + 1, count)
    dx, tail, rim, packed, ddt = call(
        grads_kernel,
        [((T, CHANNELS), BF16), ((TAIL, CHANNELS), F32), ((TAIL, CHANNELS), BF16),
         ((share * count, 8, LANES), F32), ((HEADS, T), F32)],
        [pltpu.VMEM((8 + T, LANES), F32), pltpu.VMEM((16 + T, LANES), F32),
         pltpu.VMEM((HEADS, LANES), F32), pltpu.VMEM((T, T), F32), pltpu.VMEM((T, T), F32),
         pltpu.VMEM((T, STATE), F32), pltpu.VMEM((T, STATE), F32),
         pltpu.VMEM((2 * T + 8, HEADS), F32)],
        (*base, mixed, run, step, b, c, enter, later),
    )
    piece = (share, 8, LANES)
    total_conv, total_head, end = call(
        functools.partial(sum_kernel, (count, planes)),
        [((CONV_W + 1, CHANNELS), F32), ((3, HEADS), F32), ((TAIL, CHANNELS), BF16)],
        [pltpu.VMEM((count, *piece), F32), pltpu.VMEM(piece, F32),
         pltpu.VMEM((planes, *piece), F32), pltpu.VMEM((share * count, 8, LANES), F32),
         pltpu.VMEM((TAIL, CHANNELS), BF16)]
        + [pltpu.SemaphoreType.DMA((k,)) for k in (count, count, planes, planes, count, count, 2)],
        (packed, tail, rim),
        collective_id=1,
        has_side_effects=True,
    )
    dx = lax.dynamic_update_slice(dx, end, (T - TAIL, 0))
    return (dx[None], ddt[None], total_conv, total_head)


def solution(mesh):
    return jax.shard_map(
        shards,
        mesh=mesh,
        in_specs=(P("fsdp", "ctx", None), P("fsdp", None, "ctx"), P("fsdp", "ctx", None), P(), P()),
        out_specs=(P("fsdp", "ctx", None), P("fsdp", None, "ctx"), P(), P()),
        check_vma=False,
    )
```

time: 558 us -> 172 us (0.31); the launches traced: 548 us -> 172 us
  waiting for transfers between devices: 194 us -> 1.39 us
  Pallas kernels: 0 us -> 160 us
  other arithmetic: 125 us -> 0 us
  matrix products: 85.6 us -> 0 us
  blocking collectives: 78.8 us -> 0 us
  local copies, waits for them, and re-layouts: 43.4 us -> 6.3 us
  between operations: 14.8 us -> 0.66 us
    pallas_call x0 -> x4, Pallas kernels: none -> 160 us  [call(): pl.pallas_call(kernel, out_shape=[jax.ShapeDtypeStruct(s, d) for s, d in...]
    all_gather x2 -> x0, waiting for transfers between devices: 118 us -> none  [entering_2(): lax.all_gather(a.astype(kind), axis)]
    dot_general x15 -> x0, matrix products: 85.6 us -> none  [the longest x2 21.4 us: advance(): jnp.einsum('gkts,sgkp->tgkp', weights, x_grouped, precision=exact_prec)]
    psum x1 -> x0, waiting for transfers between devices: 75.8 us -> none  [shards(): total_conv, total_head = lax.psum((grad_conv, grad_head), ('ctx', 'fsdp'))]
    psum x1 -> x0, blocking collectives: 71.3 us -> none  [shards(): total_conv, total_head = lax.psum((grad_conv, grad_head), ('ctx', 'fsdp'))]
    add x8 -> x0, other arithmetic: 37.9 us -> none  [the longest x7 37.9 us: combine_carry(): later_pair[0][:, None, None] * earlier_pair[1] + later_pair[1]]
    reduce_sum x6 -> x0, other arithmetic: 35.1 us -> none  [the longest x1 21 us: prepare(): conv_params[offset][None, :] * extended[offset:offset + row_count]]
    mul x4 -> x0, other arithmetic: 19.3 us -> none  [the longest x1 12.4 us: prepare(): activated = jax.nn.silu(mixed_in)]
  transfers between devices with their start and end apart: 5 -> 1, of which waited for: 3 -> 1; matrix products, arithmetic and copies ran while one was open for 15% -> 0% of each run, Pallas kernels for 0% -> 0%
where the time goes in v1:
time: 172 us
  Pallas kernels  160 us (93%)
  local copies, waits for them, and re-layouts  6.3 us (4%)
  starting transfers between devices  3.68 us (2%)
    pallas_call x4, Pallas kernels, call(): pl.pallas_call(kernel, out_shape=[jax.ShapeDtypeStruct(s, d) for s, d in...  160 us
    ppermute x1, starting transfers between devices, shifted(): return lax.ppermute(block, axis, route)  3.68 us
  transfers between devices with their start and end apart: 1, of which 1 were waited for; matrix products, arithmetic and copies ran while one was open for 0% of the time, Pallas kernels for 0%

profile of v1, /device:TPU:25, one launch (start us, length us, event | category | flops | bytes accessed | tf_op | source)
XLA Modules:
  0.0 171.6 jit_solution(1732829550521346030)
XLA Ops:
  0.6 1.0 slice_bitcast_fusion
  1.6 3.7 %collective-permute-start = (bf16[3,9216]{1,0:T(4,128)(2,1)S(1)}, bf16[3,9216]{1,0:T(4,128)(2,1)S(1)}, u32[]{:S(2)}, u32[]{:S(2)}) collective-permute-start(bf16[3,9216]{1,0:T(4,128)(2,1)S(1)} %slice_bitcast_fusion), channel_id=1, source_target_pairs={{0,4},{4,8},{8,12},{12,16},{16,20},{20,24},{24,28},{1,5},{5,9},{9,... | collective-permute-start | bytes 165896 | tf_op jit(solution)/shard_map/ppermute | solution.py:423
  5.3 1.4 collective-permute-done
  6.7 0.7 pad.4.halo_ref
  7.4 27.5 %shard_map.84 = (f32[128,9216]{1,0:T(8,128)}, f32[8192,128]{1,0:T(8,128)}, f32[8192,128]{1,0:T(8,128)}, f32[128,128]{1,0:T(8,128)}, f32[128,128]{1,0:T(8,128)}, ...) custom-call(bf16[128,9216]{1,0:T(8,128)(2,1)} %bitcast.9, bf16[8,9216]{1,0:T(8,128)(2,1)} %pad.4.halo_ref, ...), custom_call_target="tpu_custom_call" | custom-call | tf_op jit(solution)/shard_map/pallas_call | solution.py:410
  34.9 62.5 %shard_map.85 = (bf16[8192,128]{1,0:T(8,128)(2,1)}, bf16[8192,128]{1,0:T(8,128)(2,1)}) custom-call(f32[8192,128]{1,0:T(8,128)} %get-tuple-element.27.leave_ref, f32[8192,128]{1,0:T(8,128)} %get-tuple-element.28.pull_ref, f32[128,128]{1,0:T(8,128)} %get-tuple-element.29.fade_ref), custom_call_target="tpu_custom_call" | custom-call | tf_op jit(solution)/shard_map/pallas_call | solution.py:410
  97.4 46.0 %shard_map.86 = (bf16[128,9216]{1,0:T(8,128)(2,1)}, f32[16,9216]{1,0:T(8,128)}, bf16[16,9216]{1,0:T(8,128)(2,1)}, f32[80,8,128]{2,1,0:T(8,128)}, f32[128,128]{1,0:T(8,128)}) custom-call(bf16[128,9216]{1,0:T(8,128)(2,1)} %bitcast.10, bf16[8,9216]{1,0:T(8,128)(2,1)} %pad.4.halo_ref, bf16[128,128]{1,0:T(8,128)(2,1)} %bitcast.14, bf16[128,8192]{1,0:T(8,128)(2,1)} %bitcast.12, ...), custom_call_target="tpu_custom_call" | custom-call | tf_op jit(solution)/shard_map/pallas_call | solution.py:410
  143.4 23.6 %shard_map.87 = (f32[5,9216]{1,0:T(8,128)}, f32[3,128]{1,0:T(4,128)}, bf16[16,9216]{1,0:T(8,128)(2,1)}) custom-call(f32[80,8,128]{2,1,0:T(8,128)} %get-tuple-element.33.packed_ref, f32[16,9216]{1,0:T(8,128)} %get-tuple-element.34.tail_ref, bf16[16,9216]{1,0:T(8,128)(2,1)} %get-tuple-element.35.rim_ref), custom_call_target="tpu_custom_call" | custom-call | tf_op jit(solution)/shard_map/pallas_call | solution.py:410
  167.0 1.7 bitcast_dynamic-update-slice_fusion
  168.7 1.7 copy.12
  170.4 1.2 copy.13
Async XLA Ops:
  1.6 5.1 %collective-permute-start = (bf16[3,9216]{1,0:T(4,128)(2,1)S(1)}, bf16[3,9216]{1,0:T(4,128)(2,1)S(1)}, u32[]{:S(2)}, u32[]{:S(2)}) collective-permute-start(bf16[3,9216]{1,0:T(4,128)(2,1)S(1)} %slice_bitcast_fusion), channel_id=1, source_target_pairs={{0,4},{4,8},{8,12},{12,16},{16,20},{20,24},{24,28},{1,5},{5,9},{9,... | collective-permute-start | bytes 165896 | tf_op jit(solution)/shard_map/ppermute | solution.py:423

commit v2 on v1

--- a/solution.py
+++ b/solution.py
@@ -59,11 +59,20 @@
     return jnp.concatenate([top, low], axis=0).T
 
 
-def states_kernel(
+def main_kernel(
+    count,
     xbc_ref, halo_ref, dt_ref, dy_ref, conv_ref, head_ref,
-    mixed_ref, leave_ref, pull_ref, fade_ref, run_ref, step_ref, b_ref, c_ref,
-    ext,
+    dx_ref, tail_ref, rim_ref, packed_ref, ddt_ref,
+    ext, dms, mixed_ref, xd_ref, y_ref, dxd_ref, leave_ref, pull_ref,
+    out_f, out_b, in_f, in_b, fade_ref, run_ref, step_ref, skip_ref, b_ref, c_ref,
+    scores, dscores, db, dc, acc, send_f, recv_f, send_b, recv_b,
 ):
+    me = lax.axis_index("ctx")
+    barrier = pltpu.get_barrier_semaphore()
+    first, last = me == 0, me == count - 1
+    for peer in (lax.rem(me + 1, count), lax.rem(me + count - 1, count)):
+        pl.semaphore_signal(barrier, inc=1, device_id={"ctx": peer}, device_id_type=MESH)
+
     step_th = softplus(dt_ref[...].astype(F32).T + head_ref[0:1, :])
     rate_th = step_th * jnp.exp(head_ref[1:2, :])
     lower = (iota2((T, T), 0) >= iota2((T, T), 1)).astype(F32)
@@ -71,46 +80,58 @@
     run_ref[...] = run_ht
     step_ref[...] = step_th.T
     fade_ref[...] = jnp.broadcast_to(jnp.exp(-run_ht[:, T - 1 : T]), (HEADS, LANES))
+    skip_ref[...] = jnp.broadcast_to(head_ref[2:3, :], (LANES, HEADS)).T
+    acc[...] = jnp.zeros_like(acc)
+    packed_ref[...] = jnp.zeros_like(packed_ref)
+    dscores[...] = jnp.zeros_like(dscores)
+    for slot in range(2):
+        dms[slot, 0:8, :] = jnp.zeros((8, LANES), F32)
+        dms[slot, 8 + T : 16 + T, :] = jnp.zeros((8, LANES), F32)
+    causal = iota2((T, T), 0) >= iota2((T, T), 1)
+    left = iota2((T, LANES), 1) < HEAD_DIM
+    zero = jnp.zeros((T, LANES), BF16)
+
+    def split(v):
+        return jnp.concatenate([jnp.where(left, v, zero), jnp.where(left, zero, v)], 0)
 
     def convolve(i):
         cols = block_of(i)
-        ext[0:8, :] = halo_ref[:, cols].astype(F32)
-        ext[8 : 8 + T, :] = xbc_ref[:, cols].astype(F32)
-        mixed = conv_ref[CONV_W : CONV_W + 1, cols] + conv_ref[0:1, cols] * ext[5 : 5 + T, :]
+        ext[0:8, cols] = halo_ref[:, cols].astype(F32)
+        ext[8 : 8 + T, cols] = xbc_ref[:, cols].astype(F32)
+        mixed = conv_ref[CONV_W : CONV_W + 1, cols] + conv_ref[0:1, cols] * ext[5 : 5 + T, cols]
         for j in range(1, CONV_W):
-            mixed = mixed + conv_ref[j : j + 1, cols] * ext[5 + j : 5 + j + T, :]
+            mixed = mixed + conv_ref[j : j + 1, cols] * ext[5 + j : 5 + j + T, cols]
         mixed_ref[:, cols] = mixed
         return mixed * sigmoid(mixed)
 
     def bc(g, _):
-        b_ref[:, block_of(g)] = convolve(PAIRS + g).astype(BF16)
-        c_ref[:, block_of(g)] = convolve(PAIRS + GROUPS + g).astype(BF16)
+        b16 = convolve(PAIRS + g).astype(BF16)
+        c16 = convolve(PAIRS + GROUPS + g).astype(BF16)
+        b_ref[:, block_of(g)] = b16
+        c_ref[:, block_of(g)] = c16
+        scores[g] = dot(c16, b16, 1, 1)
         return 0
 
     lax.fori_loop(0, GROUPS, bc, 0)
 
-    def pair(i, _):
+    def states(i):
         g = i // PER_GROUP
         x = convolve(i)
         run = wide_pair(run_ref, 2 * i)
-        step = wide_pair(step_ref, 2 * i)
-        tail = (x * step * jnp.exp(run - run[T - 1 : T, :])).astype(BF16)
+        xd = (x * wide_pair(step_ref, 2 * i)).astype(BF16)
+        xd_ref[:, block_of(i)] = xd
+        tail = (xd.astype(F32) * jnp.exp(run - run[T - 1 : T, :])).astype(BF16)
         out = (jnp.exp(-run) * dy_ref[:, block_of(i)].astype(F32)).astype(BF16)
         leave_ref[block_of(i), :] = dot(tail, b_ref[:, block_of(g)], 0, 0)
         pull_ref[block_of(i), :] = dot(out, c_ref[:, block_of(g)], 0, 0)
+
+    def states_two(k, _):
+        states(2 * k)
+        states(2 * k + 1)
         return 0
 
-    lax.fori_loop(0, PAIRS, pair, 0)
-
-
-def chain_kernel(count, leave_ref, pull_ref, fade_ref, enter_ref, later_ref,
-                 out_f, out_b, in_f, in_b, send_f, recv_f, send_b, recv_b):
-    me = lax.axis_index("ctx")
-    barrier = pltpu.get_barrier_semaphore()
-    first, last = me == 0, me == count - 1
-
-    for peer in (lax.rem(me + 1, count), lax.rem(me + count - 1, count)):
-        pl.semaphore_signal(barrier, inc=1, device_id={"ctx": peer}, device_id_type=MESH)
+    lax.fori_loop(0, PAIRS // 2, states_two, 0)
+
     pl.semaphore_wait(barrier, 2)
 
     def rows_of(c):
@@ -123,132 +144,110 @@
             device_id={"ctx": peer}, device_id_type=MESH,
         )
 
-    def handle(c, own, src, dst, send, recv, peer, begins, ends, result):
+    def handle(c, own, src, dst, send, recv, peer, begins, ends):
         @pl.when(begins)
         def _():
-            result[rows_of(c), :] = jnp.zeros((CHUNK_ROWS, LANES), BF16)
+            dst[rows_of(c), :] = jnp.zeros((CHUNK_ROWS, LANES), BF16)
 
         @pl.when(jnp.logical_not(begins))
         def _():
             copy(c, src, dst, send, recv, peer).wait_recv()
-            result[rows_of(c), :] = dst[rows_of(c), :]
 
         @pl.when(jnp.logical_not(ends))
         def _():
             for k in range(CHUNK_HEADS):
                 rows = pl.ds(pl.multiple_of(c * CHUNK_ROWS + k * HEAD_DIM, HEAD_DIM), HEAD_DIM)
                 fade = fade_ref[pl.ds(c * CHUNK_HEADS + k, 1), :]
-                src[rows, :] = (fade * result[rows, :].astype(F32) + own[rows, :]).astype(BF16)
+                src[rows, :] = (fade * dst[rows, :].astype(F32) + own[rows, :]).astype(BF16)
             copy(c, src, dst, send, recv, peer).start()
 
     up = jnp.minimum(me + 1, count - 1)
     down = jnp.maximum(me - 1, 0)
+    ticks = CHUNKS + (count - 1) * LAG
+    load = pl.cdiv(PAIRS, ticks)
+
+    def inner(i):
+        h = 2 * i
+        g = i // PER_GROUP
+        cols = block_of(i)
+        fades = []
+        for k in range(2):
+            row = jnp.broadcast_to(run_ref[pl.ds(h + k, 1), :], (T, T))
+            fades.append(jnp.exp(jnp.where(causal, row - row.T, -1e30)))
+        dy16 = dy_ref[:, cols]
+        bd_x = split(xd_ref[:, cols])
+        sc = scores[g]
+        w = [(sc * f).astype(BF16) for f in fades]
+        y_ref[:, cols] = dot(jnp.concatenate(w, 1), bd_x, 1, 0)
+        dxd_ref[:, cols] = dot(jnp.concatenate(w, 0), split(dy16), 0, 0)
+        pairwise = dot(dy16, bd_x, 1, 1)
+        dscores[g] += pairwise[:, :T] * fades[0] + pairwise[:, T:] * fades[1]
 
     def tick(v, _):
         c = v - me * LAG
 
         @pl.when(jnp.logical_and(c >= 0, c < CHUNKS))
         def _():
-            handle(c, leave_ref, out_f, in_f, send_f, recv_f, up, first, last, enter_ref)
+            handle(c, leave_ref, out_f, in_f, send_f, recv_f, up, first, last)
 
         d = v - (count - 1 - me) * LAG
 
         @pl.when(jnp.logical_and(d >= 0, d < CHUNKS))
         def _():
-            handle(d, pull_ref, out_b, in_b, send_b, recv_b, down, last, first, later_ref)
+            handle(d, pull_ref, out_b, in_b, send_b, recv_b, down, last, first)
+
+        @pl.when((v + 1) * load <= PAIRS)
+        def _():
+            for k in range(load):
+                inner(v * load + k)
 
         return 0
 
-    lax.fori_loop(0, CHUNKS + (count - 1) * LAG, tick, 0)
-
-    def drain(c, _):
-        @pl.when(jnp.logical_not(last))
-        def _():
-            copy(c, out_f, in_f, send_f, recv_f, up).wait_send()
-
-        @pl.when(jnp.logical_not(first))
-        def _():
-            copy(c, out_b, in_b, send_b, recv_b, down).wait_send()
-
-        return 0
-
-    lax.fori_loop(0, CHUNKS, drain, 0)
-
-
-def grads_kernel(
-    xbc_ref, halo_ref, dt_ref, dy_ref, conv_ref, head_ref,
-    mixed_ref, run_ref, step_ref, b_ref, c_ref, enter_ref, later_ref,
-    dx_ref, tail_ref, rim_ref, packed_ref, ddt_ref,
-    ext, dms, skip_ref, scores, dscores, db, dc, acc,
-):
-    skip_ref[...] = jnp.broadcast_to(head_ref[2:3, :], (LANES, HEADS)).T
-    acc[...] = jnp.zeros_like(acc)
-    packed_ref[...] = jnp.zeros_like(packed_ref)
-    dms[0:8, :] = jnp.zeros((8, LANES), F32)
-    dms[8 + T : 16 + T, :] = jnp.zeros((8, LANES), F32)
-    causal = iota2((T, T), 0) >= iota2((T, T), 1)
-    lane = iota2((T, LANES), 1)
-    left = lane < HEAD_DIM
-
-    def conv_back(i, mixed, sig, dact):
+    lax.fori_loop(0, ticks, tick, 0)
+    for i in range(PAIRS // load * load, PAIRS):
+        inner(i)
+
+    def conv_back(i, slot, mixed, sig, dact):
         cols = block_of(i)
         dm = dact * (sig * (1.0 + mixed * (1.0 - sig)))
-        dms[8 : 8 + T, :] = dm
-        ext[0:8, :] = halo_ref[:, cols].astype(F32)
-        ext[8 : 8 + T, :] = xbc_ref[:, cols].astype(F32)
+        dms[slot, 8 : 8 + T, :] = dm
         taps = [conv_ref[j : j + 1, cols] for j in range(CONV_W)]
         own = taps[3] * dm
-        rim = taps[0] * dms[8:16, :]
+        rim = taps[0] * dms[slot, 8:16, :]
         for j in range(3):
-            own = own + taps[j] * dms[11 - j : 11 - j + T, :]
+            own = own + taps[j] * dms[slot, 11 - j : 11 - j + T, :]
         for j in range(1, 3):
-            rim = rim + taps[j] * dms[8 - j : 16 - j, :]
+            rim = rim + taps[j] * dms[slot, 8 - j : 16 - j, :]
         dx_ref[:, cols] = own.astype(BF16)
         tail_ref[:, cols] = own[T - TAIL :, :]
         rim_ref[:, cols] = jnp.concatenate([rim, jnp.zeros_like(rim)], 0).astype(BF16)
         for j in range(CONV_W):
-            packed_ref[i, j : j + 1, :] = jnp.sum(dm * ext[5 + j : 5 + j + T, :], 0, keepdims=True)
+            packed_ref[i, j : j + 1, :] = jnp.sum(
+                dm * ext[5 + j : 5 + j + T, cols], 0, keepdims=True
+            )
         packed_ref[i, CONV_W : CONV_W + 1, :] = jnp.sum(dm, 0, keepdims=True)
 
-    def pair(i, g):
+    def pair(i, g, slot):
         h = 2 * i
         cols = block_of(i)
         mixed = mixed_ref[:, cols]
         sig = sigmoid(mixed)
         x = mixed * sig
-        dy16 = dy_ref[:, cols]
-        dy = dy16.astype(F32)
+        dy = dy_ref[:, cols].astype(F32)
         step = wide_pair(step_ref, h)
-        fades = []
-        runs = []
-        for k in range(2):
-            row = jnp.broadcast_to(run_ref[pl.ds(h + k, 1), :], (T, T))
-            col = row.T
-            runs.append(col)
-            fades.append(jnp.exp(jnp.where(causal, row - col, -1e30)))
-        run = jnp.where(left, runs[0], runs[1])
-        xd16 = (x * step).astype(BF16)
-        xd = xd16.astype(F32)
+        run = wide_pair(run_ref, h)
+        xd = xd_ref[:, cols].astype(F32)
         e_tail = jnp.exp(run - run[T - 1 : T, :])
         e_head = jnp.exp(-run)
-        zero = jnp.zeros((T, LANES), BF16)
-        bd_x = jnp.concatenate([jnp.where(left, xd16, zero), jnp.where(left, zero, xd16)], 0)
-        bd_y = jnp.concatenate([jnp.where(left, dy16, zero), jnp.where(left, zero, dy16)], 0)
-        sc = scores[...]
-        w = [(sc * f).astype(BF16) for f in fades]
-        enter = enter_ref[cols, :]
-        later = later_ref[cols, :]
-        b16 = b_ref[:, block_of(g)]
-        c16 = c_ref[:, block_of(g)]
-        y = dot(jnp.concatenate(w, 1), bd_x, 1, 0) + e_head * dot(c16, enter, 1, 1)
-        from_tail = e_tail * dot(b16, later, 1, 1)
-        dxd = dot(jnp.concatenate(w, 0), bd_y, 0, 0) + from_tail
-        pairwise = dot(dy16, bd_x, 1, 1)
-        dscores[...] += pairwise[:, :T] * fades[0] + pairwise[:, T:] * fades[1]
+        enter = in_f[cols, :]
+        later = in_b[cols, :]
+        y = y_ref[:, cols] + e_head * dot(c_ref[:, block_of(g)], enter, 1, 1)
+        from_tail = e_tail * dot(b_ref[:, block_of(g)], later, 1, 1)
+        dxd = dxd_ref[:, cols] + from_tail
         dc[...] += dot((e_head * dy).astype(BF16), enter, 1, 0)
         db[...] += dot((xd * e_tail).astype(BF16), later, 1, 0)
         skip = jnp.where(left[0:1, :], skip_ref[pl.ds(h, 1), :], skip_ref[pl.ds(h + 1, 1), :])
-        conv_back(i, mixed, sig, step * dxd + skip * dy)
+        conv_back(i, slot, mixed, sig, step * dxd + skip * dy)
         both = (enter.astype(F32) * later.astype(F32)).astype(BF16)
         passed = dot(jnp.ones((8, STATE), BF16), both, 1, 1)
         sub = iota2((8, LANES), 0)
@@ -267,25 +266,24 @@
         )
 
     def group(g, _):
+        db[...] = jnp.zeros_like(db)
+        dc[...] = jnp.zeros_like(dc)
+
+        def two(k, _):
+            pair(g * PER_GROUP + 2 * k, g, 0)
+            pair(g * PER_GROUP + 2 * k + 1, g, 1)
+            return 0
+
+        lax.fori_loop(0, PER_GROUP // 2, two, 0)
+        ds = dscores[g].astype(BF16)
         b16 = b_ref[:, block_of(g)]
         c16 = c_ref[:, block_of(g)]
-        scores[...] = dot(c16, b16, 1, 1)
-        dscores[...] = jnp.zeros_like(dscores)
-        db[...] = jnp.zeros_like(db)
-        dc[...] = jnp.zeros_like(dc)
-
-        def inner(k, _):
-            pair(g * PER_GROUP + k, g)
-            return 0
-
-        lax.fori_loop(0, PER_GROUP, inner, 0)
-        ds = dscores[...].astype(BF16)
-        for at, total in (
-            (PAIRS + g, db[...] + dot(ds, c16, 0, 0)),
-            (PAIRS + GROUPS + g, dc[...] + dot(ds, b16, 1, 0)),
+        for slot, at, total in (
+            (0, PAIRS + g, db[...] + dot(ds, c16, 0, 0)),
+            (1, PAIRS + GROUPS + g, dc[...] + dot(ds, b16, 1, 0)),
         ):
             mixed = mixed_ref[:, block_of(at)]
-            conv_back(at, mixed, sigmoid(mixed), total)
+            conv_back(at, slot, mixed, sigmoid(mixed), total)
         return 0
 
     lax.fori_loop(0, GROUPS, group, 0)
@@ -299,6 +297,19 @@
     packed_ref[BLOCKS, 0:1, :] = jnp.sum(d_dt, 0, keepdims=True)
     packed_ref[BLOCKS, 1:2, :] = jnp.sum(d_rate * softplus(raw) * scale, 0, keepdims=True)
     packed_ref[BLOCKS, 2:3, :] = acc[2 * T : 2 * T + 1, :]
+
+    def drain(c, _):
+        @pl.when(jnp.logical_not(last))
+        def _():
+            copy(c, out_f, in_f, send_f, recv_f, up).wait_send()
+
+        @pl.when(jnp.logical_not(first))
+        def _():
+            copy(c, out_b, in_b, send_b, recv_b, down).wait_send()
+
+        return 0
+
+    lax.fori_loop(0, CHUNKS, drain, 0)
 
 
 def sum_kernel(
@@ -429,36 +440,26 @@
     x = xbc[0]
     halo = jnp.pad(shifted(x[T - rim_rows :], "ctx", 1), ((8 - rim_rows, 0), (0, 0)))
     base = (x, halo, dt_raw[0], dy[0], conv_params, head_params)
-    bc_width = GROUPS * STATE
-    mixed, leave, pull, fade, run, step, b, c = call(
-        states_kernel,
-        [((T, CHANNELS), F32), ((X_WIDTH, STATE), F32), ((X_WIDTH, STATE), F32),
-         ((HEADS, LANES), F32), ((HEADS, T), F32), ((HEADS, T), F32),
-         ((T, bc_width), BF16), ((T, bc_width), BF16)],
-        [pltpu.VMEM((8 + T, LANES), F32)],
+    planes = lax.axis_size("fsdp")
+    share = pl.cdiv(BLOCKS + 1, count)
+    wide, wide16 = pltpu.VMEM((T, X_WIDTH), F32), pltpu.VMEM((T, X_WIDTH), BF16)
+    tall, tall16 = pltpu.VMEM((X_WIDTH, STATE), F32), pltpu.VMEM((X_WIDTH, STATE), BF16)
+    small = pltpu.VMEM((T, LANES), F32)
+    narrow = pltpu.VMEM((T, GROUPS * STATE), BF16)
+    square = pltpu.VMEM((GROUPS, T, T), F32)
+    dx, tail, rim, packed, ddt = call(
+        functools.partial(main_kernel, count),
+        [((T, CHANNELS), BF16), ((TAIL, CHANNELS), F32), ((TAIL, CHANNELS), BF16),
+         ((share * count, 8, LANES), F32), ((HEADS, T), F32)],
+        [pltpu.VMEM((8 + T, CHANNELS), F32), pltpu.VMEM((2, 16 + T, LANES), F32),
+         pltpu.VMEM((T, CHANNELS), F32), wide16, wide, wide, tall, tall,
+         tall16, tall16, tall16, tall16, small, small, small, small, narrow, narrow,
+         square, square, small, small, pltpu.VMEM((2 * T + 8, HEADS), F32)]
+        + [pltpu.SemaphoreType.DMA((CHUNKS,))] * 4,
         base,
-    )
-    wire = pltpu.VMEM((X_WIDTH, STATE), BF16)
-    sems = pltpu.SemaphoreType.DMA((CHUNKS,))
-    enter, later = call(
-        functools.partial(chain_kernel, count),
-        [((X_WIDTH, STATE), BF16)] * 2,
-        [wire, wire, wire, wire, sems, sems, sems, sems],
-        (leave, pull, fade),
+        limit=60,
         collective_id=0,
         has_side_effects=True,
-    )
-    planes = lax.axis_size("fsdp")
-    share = pl.cdiv(BLOCKS + 1, count)
-    dx, tail, rim, packed, ddt = call(
-        grads_kernel,
-        [((T, CHANNELS), BF16), ((TAIL, CHANNELS), F32), ((TAIL, CHANNELS), BF16),
-         ((share * count, 8, LANES), F32), ((HEADS, T), F32)],
-        [pltpu.VMEM((8 + T, LANES), F32), pltpu.VMEM((16 + T, LANES), F32),
-         pltpu.VMEM((HEADS, LANES), F32), pltpu.VMEM((T, T), F32), pltpu.VMEM((T, T), F32),
-         pltpu.VMEM((T, STATE), F32), pltpu.VMEM((T, STATE), F32),
-         pltpu.VMEM((2 * T + 8, HEADS), F32)],
-        (*base, mixed, run, step, b, c, enter, later),
     )
     piece = (share, 8, LANES)
     total_conv, total_head, end = call(

time: 172 us -> 140 us (0.81)
  Pallas kernels: 160 us -> 125 us
  local copies, waits for them, and re-layouts: 6.3 us -> 8.56 us
    pallas_call x4 -> x2, Pallas kernels: 160 us -> 125 us  [call(): pl.pallas_call(kernel, out_shape=[jax.ShapeDtypeStruct(s, d) for s, d in...]
    unnamed x2 -> x10, local copies, waits for them, and re-layouts: 2.94 us -> 5.2 us
where the time goes in v2:
time: 140 us
  Pallas kernels  125 us (89%)
  local copies, waits for them, and re-layouts  8.56 us (6%)
  starting transfers between devices  3.68 us (3%)
    pallas_call x2, Pallas kernels, call(): pl.pallas_call(kernel, out_shape=[jax.ShapeDtypeStruct(s, d) for s, d in...  125 us
    unnamed x10, local copies, waits for them, and re-layouts  5.2 us
    ppermute x1, starting transfers between devices, shifted(): return lax.ppermute(block, axis, route)  3.68 us
  transfers between devices with their start and end apart: 1, of which 1 were waited for; matrix products, arithmetic and copies ran while one was open for 0% of the time, Pallas kernels for 0%

profile of v2, /device:TPU:25, one launch (start us, length us, event | category | flops | bytes accessed | tf_op | source)
XLA Modules:
  0.0 139.8 jit_solution(17110700188589681458)
XLA Ops:
  0.6 1.0 slice_bitcast_fusion
  1.6 3.7 %collective-permute-start = (bf16[3,9216]{1,0:T(4,128)(2,1)S(1)}, bf16[3,9216]{1,0:T(4,128)(2,1)S(1)}, u32[]{:S(2)}, u32[]{:S(2)}) collective-permute-start(bf16[3,9216]{1,0:T(4,128)(2,1)S(1)} %slice_bitcast_fusion), channel_id=1, source_target_pairs={{0,4},{4,8},{8,12},{12,16},{16,20},{20,24},{24,28},{1,5},{5,9},{9,... | collective-permute-start | bytes 165896 | tf_op jit(solution)/shard_map/ppermute | solution.py:434
  5.3 1.4 collective-permute-done
  6.7 0.7 pad.4.halo_ref
  7.4 101.1 %shard_map.84 = (bf16[128,9216]{1,0:T(8,128)(2,1)}, f32[16,9216]{1,0:T(8,128)}, bf16[16,9216]{1,0:T(8,128)(2,1)}, f32[80,8,128]{2,1,0:T(8,128)}, f32[128,128]{1,0:T(8,128)}) custom-call(bf16[128,9216]{1,0:T(8,128)(2,1)} %bitcast.9, bf16[8,9216]{1,0:T(8,128)(2,1)} %pad.4.halo_ref, bf16[128,128]{1,0:T(8,128)(2,1)} %bitcast.13, bf16[128,8192]{1,0:T(8,128)(2,1)} %bitcast.11, ...), custom_call_target="tpu_custom_call" | custom-call | tf_op jit(solution)/shard_map/pallas_call | solution.py:421
  108.5 24.4 %shard_map.85 = (f32[5,9216]{1,0:T(8,128)}, f32[3,128]{1,0:T(4,128)}, bf16[16,9216]{1,0:T(8,128)(2,1)}) custom-call(f32[80,8,128]{2,1,0:T(8,128)} %get-tuple-element.13.packed_ref, f32[16,9216]{1,0:T(8,128)} %get-tuple-element.14.tail_ref, bf16[16,9216]{1,0:T(8,128)(2,1)} %get-tuple-element.15.rim_ref), custom_call_target="tpu_custom_call" | custom-call | tf_op jit(solution)/shard_map/pallas_call | solution.py:421
  132.9 1.7 %bitcast_dynamic-update-slice_fusion = bf16[1,128,9216]{2,1,0:T(8,128)(2,1)} fusion(bf16[1,128,9216]{2,1,0:T(8,128)(2,1)} %bitcast.10, bf16[16,9216]{1,0:T(8,128)(2,1)} %get-tuple-element.16), kind=kLoop, calls=%fused_computation | loop fusion | bytes 589824 | tf_op jit(solution)/shard_map/dynamic_update_slice | solution.py:476
  134.6 0.0 copy-start.1
  134.6 0.0 copy-start
  134.6 0.0 copy-start.2
  134.6 3.3 %copy.14 = bf16[1,128,9216]{2,1,0:T(8,128)(2,1)} copy(bf16[1,128,9216]{2,1,0:T(8,128)(2,1)} %bitcast_dynamic-update-slice_fusion) | data formatting | bytes 4718592
  137.8 0.0 copy-done.1
  137.8 0.6 copy.15
  138.5 0.0 copy-done
  138.5 0.7 copy.16
  139.2 0.0 copy-done.2
  139.2 0.6 copy.17
Async XLA Ops:
  1.6 5.1 %collective-permute-start = (bf16[3,9216]{1,0:T(4,128)(2,1)S(1)}, bf16[3,9216]{1,0:T(4,128)(2,1)S(1)}, u32[]{:S(2)}, u32[]{:S(2)}) collective-permute-start(bf16[3,9216]{1,0:T(4,128)(2,1)S(1)} %slice_bitcast_fusion), channel_id=1, source_target_pairs={{0,4},{4,8},{8,12},{12,16},{16,20},{20,24},{24,28},{1,5},{5,9},{9,... | collective-permute-start | bytes 165896 | tf_op jit(solution)/shard_map/ppermute | solution.py:434
  134.6 3.3 %copy-start.1 = (f32[128,128]{1,0:T(8,128)S(1)}, f32[128,128]{1,0:T(8,128)}, u32[]{:S(2)}) copy-start(f32[128,128]{1,0:T(8,128)} %get-tuple-element.17) | copy-start | bytes 196612
  134.6 3.9 %copy-start = (f32[5,9216]{1,0:T(8,128)S(1)}, f32[5,9216]{1,0:T(8,128)}, u32[]{:S(2)}) copy-start(f32[5,9216]{1,0:T(8,128)} %get-tuple-element.26) | copy-start | bytes 552964
  134.6 4.6 %copy-start.2 = (f32[3,128]{1,0:T(4,128)S(1)}, f32[3,128]{1,0:T(4,128)}, u32[]{:S(2)}) copy-start(f32[3,128]{1,0:T(4,128)} %get-tuple-element.27) | copy-start | bytes 4612

commit v3 on v2

--- a/solution.py
+++ b/solution.py
@@ -21,10 +21,10 @@
 F32 = jnp.float32
 BF16 = jnp.bfloat16
 MESH = pl.DeviceIdType.MESH
-CHUNKS = 16
+CHUNKS = 32
 CHUNK_HEADS = HEADS // CHUNKS
 CHUNK_ROWS = X_WIDTH // CHUNKS
-LAG = 2
+LAG = 3
 TAIL = 16
 BLOCKS = CHANNELS // LANES
 
@@ -125,13 +125,6 @@
         leave_ref[block_of(i), :] = dot(tail, b_ref[:, block_of(g)], 0, 0)
         pull_ref[block_of(i), :] = dot(out, c_ref[:, block_of(g)], 0, 0)
 
-    def states_two(k, _):
-        states(2 * k)
-        states(2 * k + 1)
-        return 0
-
-    lax.fori_loop(0, PAIRS // 2, states_two, 0)
-
     pl.semaphore_wait(barrier, 2)
 
     def rows_of(c):
@@ -164,7 +157,9 @@
     up = jnp.minimum(me + 1, count - 1)
     down = jnp.maximum(me - 1, 0)
     ticks = CHUNKS + (count - 1) * LAG
-    load = pl.cdiv(PAIRS, ticks)
+    later_ticks = ticks - CHUNKS
+    load = pl.cdiv(PAIRS, later_ticks)
+    per_chunk = PAIRS // CHUNKS
 
     def inner(i):
         h = 2 * i
@@ -184,6 +179,11 @@
         dscores[g] += pairwise[:, :T] * fades[0] + pairwise[:, T:] * fades[1]
 
     def tick(v, _):
+        @pl.when(v < CHUNKS)
+        def _():
+            for k in range(per_chunk):
+                states(v * per_chunk + k)
+
         c = v - me * LAG
 
         @pl.when(jnp.logical_and(c >= 0, c < CHUNKS))
@@ -196,10 +196,12 @@
         def _():
             handle(d, pull_ref, out_b, in_b, send_b, recv_b, down, last, first)
 
-        @pl.when((v + 1) * load <= PAIRS)
+        w = v - CHUNKS
+
+        @pl.when(jnp.logical_and(w >= 0, (w + 1) * load <= PAIRS))
         def _():
             for k in range(load):
-                inner(v * load + k)
+                inner(w * load + k)
 
         return 0
 

time: 140 us -> 126 us (0.900)
  Pallas kernels: 125 us -> 112 us
    pallas_call x2, Pallas kernels: 125 us -> 112 us  [call(): pl.pallas_call(kernel, out_shape=[jax.ShapeDtypeStruct(s, d) for s, d in...]
where the time goes in v3:
time: 126 us
  Pallas kernels  112 us (89%)
  local copies, waits for them, and re-layouts  8.56 us (7%)
  starting transfers between devices  3.68 us (3%)
  waiting for transfers between devices  1.39 us (1%)
    pallas_call x2, Pallas kernels, call(): pl.pallas_call(kernel, out_shape=[jax.ShapeDtypeStruct(s, d) for s, d in...  112 us
    unnamed x10, local copies, waits for them, and re-layouts  5.2 us
    ppermute x1, starting transfers between devices, shifted(): return lax.ppermute(block, axis, route)  3.68 us
  transfers between devices with their start and end apart: 1, of which 1 were waited for; matrix products, arithmetic and copies ran while one was open for 0% of the time, Pallas kernels for 0%

profile of v3, /device:TPU:25, one launch (start us, length us, event | category | flops | bytes accessed | tf_op | source)
XLA Modules:
  0.0 126.1 jit_solution(15291312200523161652)
XLA Ops:
  0.6 1.0 slice_bitcast_fusion
  1.6 3.7 %collective-permute-start = (bf16[3,9216]{1,0:T(4,128)(2,1)S(1)}, bf16[3,9216]{1,0:T(4,128)(2,1)S(1)}, u32[]{:S(2)}, u32[]{:S(2)}) collective-permute-start(bf16[3,9216]{1,0:T(4,128)(2,1)S(1)} %slice_bitcast_fusion), channel_id=1, source_target_pairs={{0,4},{4,8},{8,12},{12,16},{16,20},{20,24},{24,28},{1,5},{5,9},{9,... | collective-permute-start | bytes 165896 | tf_op jit(solution)/shard_map/ppermute | solution.py:436
  5.3 1.4 %collective-permute-done = bf16[3,9216]{1,0:T(4,128)(2,1)S(1)} collective-permute-done((bf16[3,9216]{1,0:T(4,128)(2,1)S(1)}, bf16[3,9216]{1,0:T(4,128)(2,1)S(1)}, u32[]{:S(2)}, u32[]{:S(2)}) %collective-permute-start) | collective-permute-done | bytes 55328 | tf_op jit(solution)/shard_map/ppermute | solution.py:436
  6.7 0.7 pad.4.halo_ref
  7.4 88.7 %shard_map.84 = (bf16[128,9216]{1,0:T(8,128)(2,1)}, f32[16,9216]{1,0:T(8,128)}, bf16[16,9216]{1,0:T(8,128)(2,1)}, f32[80,8,128]{2,1,0:T(8,128)}, f32[128,128]{1,0:T(8,128)}) custom-call(bf16[128,9216]{1,0:T(8,128)(2,1)} %bitcast.9, bf16[8,9216]{1,0:T(8,128)(2,1)} %pad.4.halo_ref, bf16[128,128]{1,0:T(8,128)(2,1)} %bitcast.13, bf16[128,8192]{1,0:T(8,128)(2,1)} %bitcast.11, ...), custom_call_target="tpu_custom_call" | custom-call | tf_op jit(solution)/shard_map/pallas_call | solution.py:423
  96.1 23.1 %shard_map.85 = (f32[5,9216]{1,0:T(8,128)}, f32[3,128]{1,0:T(4,128)}, bf16[16,9216]{1,0:T(8,128)(2,1)}) custom-call(f32[80,8,128]{2,1,0:T(8,128)} %get-tuple-element.13.packed_ref, f32[16,9216]{1,0:T(8,128)} %get-tuple-element.14.tail_ref, bf16[16,9216]{1,0:T(8,128)(2,1)} %get-tuple-element.15.rim_ref), custom_call_target="tpu_custom_call" | custom-call | tf_op jit(solution)/shard_map/pallas_call | solution.py:423
  119.2 1.7 %bitcast_dynamic-update-slice_fusion = bf16[1,128,9216]{2,1,0:T(8,128)(2,1)} fusion(bf16[1,128,9216]{2,1,0:T(8,128)(2,1)} %bitcast.10, bf16[16,9216]{1,0:T(8,128)(2,1)} %get-tuple-element.16), kind=kLoop, calls=%fused_computation | loop fusion | bytes 589824 | tf_op jit(solution)/shard_map/dynamic_update_slice | solution.py:478
  120.9 0.0 copy-start.1
  120.9 0.0 copy-start
  120.9 0.0 copy-start.2
  120.9 3.3 %copy.14 = bf16[1,128,9216]{2,1,0:T(8,128)(2,1)} copy(bf16[1,128,9216]{2,1,0:T(8,128)(2,1)} %bitcast_dynamic-update-slice_fusion) | data formatting | bytes 4718592
  124.2 0.0 copy-done.1
  124.2 0.6 copy.15
  124.8 0.0 copy-done
  124.8 0.7 copy.16
  125.6 0.0 copy-done.2
  125.6 0.6 copy.17
Async XLA Ops:
  1.6 5.1 %collective-permute-start = (bf16[3,9216]{1,0:T(4,128)(2,1)S(1)}, bf16[3,9216]{1,0:T(4,128)(2,1)S(1)}, u32[]{:S(2)}, u32[]{:S(2)}) collective-permute-start(bf16[3,9216]{1,0:T(4,128)(2,1)S(1)} %slice_bitcast_fusion), channel_id=1, source_target_pairs={{0,4},{4,8},{8,12},{12,16},{16,20},{20,24},{24,28},{1,5},{5,9},{9,... | collective-permute-start | bytes 165896 | tf_op jit(solution)/shard_map/ppermute | solution.py:436
  120.9 3.3 %copy-start.1 = (f32[128,128]{1,0:T(8,128)S(1)}, f32[128,128]{1,0:T(8,128)}, u32[]{:S(2)}) copy-start(f32[128,128]{1,0:T(8,128)} %get-tuple-element.17) | copy-start | bytes 196612
  120.9 3.9 %copy-start = (f32[5,9216]{1,0:T(8,128)S(1)}, f32[5,9216]{1,0:T(8,128)}, u32[]{:S(2)}) copy-start(f32[5,9216]{1,0:T(8,128)} %get-tuple-element.26) | copy-start | bytes 552964
  120.9 4.6 %copy-start.2 = (f32[3,128]{1,0:T(4,128)S(1)}, f32[3,128]{1,0:T(4,128)}, u32[]{:S(2)}) copy-start(f32[3,128]{1,0:T(4,128)} %get-tuple-element.27) | copy-start | bytes 4612

commit v4 on v3

--- a/solution.py
+++ b/solution.py
@@ -475,7 +475,7 @@
         collective_id=1,
         has_side_effects=True,
     )
-    dx = lax.dynamic_update_slice(dx, end, (T - TAIL, 0))
+    dx = jnp.concatenate([dx[: T - TAIL], end], axis=0)
     return (dx[None], ddt[None], total_conv, total_head)
 
 

time: 126 us -> 126 us (level)
  local copies, waits for them, and re-layouts: 8.56 us -> 5.31 us
  other arithmetic: 0 us -> 2.57 us
    unnamed x10 -> x9, local copies, waits for them, and re-layouts: 5.2 us -> 1.93 us
    broadcast_in_dim x0 -> x1, other arithmetic: none -> 2.57 us  [shards(): return (dx[None], ddt[None], total_conv, total_head)]
    slice x0 -> x1, local copies, waits for them, and re-layouts: none -> 1.71 us  [shards(): dx = jnp.concatenate([dx[:T - TAIL], end], axis=0)]
    dynamic_update_slice x1 -> x0, local copies, waits for them, and re-layouts: 1.7 us -> none  [shards(): dx = lax.dynamic_update_slice(dx, end, (T - TAIL, 0))]
where the time goes in v4:
time: 126 us; the launch traced here: 125 us
  Pallas kernels  112 us (89%)
  local copies, waits for them, and re-layouts  5.31 us (4%)
  starting transfers between devices  3.68 us (3%)
  other arithmetic  2.57 us (2%)
  waiting for transfers between devices  1.39 us (1%)
    pallas_call x2, Pallas kernels, call(): pl.pallas_call(kernel, out_shape=[jax.ShapeDtypeStruct(s, d) for s, d in...  112 us
    ppermute x1, starting transfers between devices, shifted(): return lax.ppermute(block, axis, route)  3.68 us
    broadcast_in_dim x1, other arithmetic, shards(): return (dx[None], ddt[None], total_conv, total_head)  2.57 us
  transfers between devices with their start and end apart: 1, of which 1 were waited for; matrix products, arithmetic and copies ran while one was open for 0% of the time, Pallas kernels for 0%

profile of v4, /device:TPU:25, one launch (start us, length us, event | category | flops | bytes accessed | tf_op | source)
XLA Modules:
  0.0 125.5 jit_solution(15734965078119950033)
XLA Ops:
  0.6 1.0 slice_bitcast_fusion
  1.6 3.7 %collective-permute-start = (bf16[3,9216]{1,0:T(4,128)(2,1)S(1)}, bf16[3,9216]{1,0:T(4,128)(2,1)S(1)}, u32[]{:S(2)}, u32[]{:S(2)}) collective-permute-start(bf16[3,9216]{1,0:T(4,128)(2,1)S(1)} %slice_bitcast_fusion), channel_id=1, source_target_pairs={{0,4},{4,8},{8,12},{12,16},{16,20},{20,24},{24,28},{1,5},{5,9},{9,... | collective-permute-start | bytes 165896 | tf_op jit(solution)/shard_map/ppermute | solution.py:436
  5.3 1.4 %collective-permute-done = bf16[3,9216]{1,0:T(4,128)(2,1)S(1)} collective-permute-done((bf16[3,9216]{1,0:T(4,128)(2,1)S(1)}, bf16[3,9216]{1,0:T(4,128)(2,1)S(1)}, u32[]{:S(2)}, u32[]{:S(2)}) %collective-permute-start) | collective-permute-done | bytes 55328 | tf_op jit(solution)/shard_map/ppermute | solution.py:436
  6.7 0.7 pad.4.halo_ref
  7.4 88.8 %shard_map.84 = (bf16[128,9216]{1,0:T(8,128)(2,1)}, f32[16,9216]{1,0:T(8,128)}, bf16[16,9216]{1,0:T(8,128)(2,1)}, f32[80,8,128]{2,1,0:T(8,128)}, f32[128,128]{1,0:T(8,128)}) custom-call(bf16[128,9216]{1,0:T(8,128)(2,1)} %bitcast.8, bf16[8,9216]{1,0:T(8,128)(2,1)} %pad.4.halo_ref, bf16[128,128]{1,0:T(8,128)(2,1)} %bitcast.11, bf16[128,8192]{1,0:T(8,128)(2,1)} %bitcast.9, ...), custom_call_target="tpu_custom_call" | custom-call | tf_op jit(solution)/shard_map/pallas_call | solution.py:423
  96.1 1.7 %slice.11 = bf16[112,9216]{1,0:T(8,128)(2,1)S(1)} slice(bf16[128,9216]{1,0:T(8,128)(2,1)} %get-tuple-element.12), slice={[0:112], [0:9216]} | slice | bytes 4128768 | tf_op jit(solution)/shard_map/slice | solution.py:478
  97.9 23.1 %shard_map.85 = (f32[5,9216]{1,0:T(8,128)}, f32[3,128]{1,0:T(4,128)}, bf16[16,9216]{1,0:T(8,128)(2,1)}) custom-call(f32[80,8,128]{2,1,0:T(8,128)} %get-tuple-element.13.packed_ref, f32[16,9216]{1,0:T(8,128)} %get-tuple-element.14.tail_ref, bf16[16,9216]{1,0:T(8,128)(2,1)} %get-tuple-element.15.rim_ref), custom_call_target="tpu_custom_call" | custom-call | tf_op jit(solution)/shard_map/pallas_call | solution.py:423
  121.0 0.0 copy-start.1
  121.0 0.0 copy-start
  121.0 0.0 copy-start.2
  121.0 2.6 %maximum_bitcast_fusion = bf16[1,128,9216]{2,1,0:T(8,128)(2,1)} fusion(bf16[16,9216]{1,0:T(8,128)(2,1)} %get-tuple-element.16, bf16[112,9216]{1,0:T(8,128)(2,1)S(1)} %slice.11), kind=kLoop, calls=%fused_computation | loop fusion | flops 4718592 | bytes 4718592 | tf_op jit(solution)/shard_map/broadcast_in_dim | solution.py:479
  123.6 0.0 copy-done.1
  123.6 0.6 copy.12
  124.2 0.0 copy-done
  124.2 0.7 copy.13
  124.9 0.0 copy-done.2
  124.9 0.6 copy.14
Async XLA Ops:
  1.6 5.1 %collective-permute-start = (bf16[3,9216]{1,0:T(4,128)(2,1)S(1)}, bf16[3,9216]{1,0:T(4,128)(2,1)S(1)}, u32[]{:S(2)}, u32[]{:S(2)}) collective-permute-start(bf16[3,9216]{1,0:T(4,128)(2,1)S(1)} %slice_bitcast_fusion), channel_id=1, source_target_pairs={{0,4},{4,8},{8,12},{12,16},{16,20},{20,24},{24,28},{1,5},{5,9},{9,... | collective-permute-start | bytes 165896 | tf_op jit(solution)/shard_map/ppermute | solution.py:436
  121.0 2.6 %copy-start.1 = (f32[128,128]{1,0:T(8,128)S(1)}, f32[128,128]{1,0:T(8,128)}, u32[]{:S(2)}) copy-start(f32[128,128]{1,0:T(8,128)} %get-tuple-element.17) | copy-start | bytes 196612
  121.0 3.2 %copy-start = (f32[5,9216]{1,0:T(8,128)S(1)}, f32[5,9216]{1,0:T(8,128)}, u32[]{:S(2)}) copy-start(f32[5,9216]{1,0:T(8,128)} %get-tuple-element.26) | copy-start | bytes 552964
  121.0 3.9 %copy-start.2 = (f32[3,128]{1,0:T(4,128)S(1)}, f32[3,128]{1,0:T(4,128)}, u32[]{:S(2)}) copy-start(f32[3,128]{1,0:T(4,128)} %get-tuple-element.27) | copy-start | bytes 4612
